TPU v7x, 32 devices: a whole 2x2x4 slice. The times are simulated.
32 devices in a mesh: dp: 8 (over z, y), shard: 4 (over x, core).
Axes of the slice: x: 2, y: 2, z: 4, core: 2. Of those that a mesh axis runs over, the one named last changes fastest.
Arguments:
- embedded: bfloat16 [30720, 1280], P(('dp', 'shard')), may hold values from -6 to 6
- mask_token_embedding: bfloat16 [1280], replicated, may hold values from -5 to 5
- destination: int32 [30720], P(('dp', 'shard')), may hold values from 0 to 8, as said below
- position: int32 [30720], P(('dp', 'shard')), may hold values from 0 to 79, as said below
- length: int32 [30720], P(('dp', 'shard')), may hold values from 0 to 80, as said below
- unmask_order: int32 [30720], P(('dp', 'shard')), may hold values from 0 to 79, as said below
- timestep: int32 [30720], P(('dp', 'shard')), may hold values from 0 to 80, as said below
- upstream: bfloat16 [12288, 1280], P(('dp', 'shard')), may hold values from -0.29882812 to 0.29882812
- gain_in: float32 [1280], replicated, may hold values from 0.4 to 1.6
- weight_in: bfloat16 [1280, 640], replicated, may hold values from -0.15625 to 0.15625
- gain_mid: float32 [640], replicated, may hold values from 0.4 to 1.6
- weight_conv: bfloat16 [640, 5, 640], replicated, may hold values from -0.109375 to 0.109375
- gain_out: float32 [640], replicated, may hold values from 0.4 to 1.6
- weight_out: bfloat16 [1280, 640], replicated, may hold values from -0.25 to 0.25
Outputs:
- grad_input: bfloat16 [12288, 1280], P(('dp', 'shard'))
- grad_weight_in: float32 [1280, 640], P('dp', 'shard')
- grad_weight_conv: float32 [640, 5, 640], P('dp', None, 'shard')
- grad_weight_out: float32 [1280, 640], P('dp', 'shard')
Inputs may be any that keep to these rules, and one draw needn't show every extreme that they name: 8 marks an empty slot. All slots of a sequence share one destination. Among the devices of one shard index, every destination receives exactly 384 rows, and one device sends one destination at most one sequence. A device's slots hold whole sequences one after another from its first slot, each in order of position; empty slots come last and hold 0. `length`: 0 on empty slots; equal on all slots of a sequence; every destination receives one sequence of exactly 80 residues. `unmask_order`: within each sequence a permutation of its positions; 0 on empty slots. `timestep`: equal on all slots of a sequence, from 1 to its length; 0 on empty slots.
All inputs are finite; a program needn't handle non-finite values.
Results may differ from a plain program's by a relative error of at most 0.0074.
Values may be sent and summed in bfloat16 or wider, within the bound.
A program may use at most 192 MiB of HBM per device.

v0:
```python
import jax
import jax.numpy as jnp
from jax import lax
from jax.sharding import PartitionSpec as P

KERNEL_TAPS = 5
DILATION_STEP = 16
LMAX = 80


EPS = 1e-05


def normalized_activation(values, gain_vec):
    row_mean = jnp.mean(values, axis=-1, keepdims=True)
    centred = values - row_mean
    row_var = jnp.mean(centred * centred, axis=-1, keepdims=True)
    return jax.nn.gelu(centred * lax.rsqrt(row_var + EPS) * gain_vec, approximate=False)


def raw_shift(values, offset):
    if offset > 0:
        filler = jnp.zeros((offset, values.shape[1]), values.dtype)
        return jnp.concatenate([values[offset:], filler], axis=0)
    if offset < 0:
        filler = jnp.zeros((-offset, values.shape[1]), values.dtype)
        return jnp.concatenate([filler, values[:offset]], axis=0)
    return values


def contract_rows(left, right):
    return lax.dot_general(
        left, right, (((0,), (0,)), ((), ())), preferred_element_type=jnp.float32
    )


def contract_cols(left, right):
    return lax.dot_general(
        left, right, (((1,), (1,)), ((), ())), preferred_element_type=jnp.float32
    )


def layer_grads(
    owner_input,
    upstream,
    owner_position,
    owner_length,
    gain_in,
    weight_in,
    gain_mid,
    weight_conv,
    gain_out,
    weight_out,
):
    widened_input = owner_input.astype(jnp.float32)
    first_f32, pull_in = jax.vjp(lambda value: normalized_activation(value, gain_in), widened_input)
    first_act = first_f32.astype(jnp.bfloat16)
    hidden = jnp.dot(first_act, weight_in, preferred_element_type=jnp.float32)
    mid_f32, pull_mid = jax.vjp(lambda value: normalized_activation(value, gain_mid), hidden)
    mid_act = mid_f32.astype(jnp.bfloat16)
    tap_offsets = [
        (kernel_tap_index - KERNEL_TAPS // 2) * DILATION_STEP
        for kernel_tap_index in range(KERNEL_TAPS)
    ]
    tap_valid = [
        (owner_position + offset >= 0) & (owner_position + offset < owner_length)
        for offset in tap_offsets
    ]
    tap_list = [
        jnp.where(
            tap_valid[kernel_tap_index][:, None],
            raw_shift(mid_act, tap_offsets[kernel_tap_index]),
            jnp.zeros_like(mid_act),
        )
        for kernel_tap_index in range(KERNEL_TAPS)
    ]
    conv = jnp.dot(tap_list[0], weight_conv[:, 0, :], preferred_element_type=jnp.float32)
    for kernel_tap_index in range(1, KERNEL_TAPS):
        conv = conv + jnp.dot(
            tap_list[kernel_tap_index],
            weight_conv[:, kernel_tap_index, :],
            preferred_element_type=jnp.float32,
        )
    out_f32, pull_out = jax.vjp(lambda value: normalized_activation(value, gain_out), conv)
    out_act = out_f32.astype(jnp.bfloat16)
    grad_out = contract_rows(upstream, out_act)
    out_cot = jnp.dot(upstream, weight_out, preferred_element_type=jnp.float32)
    conv_cot = pull_out(out_cot)[0].astype(jnp.bfloat16)
    grad_conv = jnp.stack(
        [
            contract_rows(tap_list[kernel_tap_index], conv_cot)
            for kernel_tap_index in range(KERNEL_TAPS)
        ],
        axis=1,
    )
    mid_cot = jnp.zeros(mid_act.shape, jnp.float32)
    for kernel_tap_index in range(KERNEL_TAPS):
        back_term = contract_cols(conv_cot, weight_conv[:, kernel_tap_index, :])
        back_term = jnp.where(
            tap_valid[kernel_tap_index][:, None], back_term, jnp.zeros_like(back_term)
        )
        mid_cot = mid_cot + raw_shift(back_term, -tap_offsets[kernel_tap_index])
    hidden_cot = pull_mid(mid_cot)[0].astype(jnp.bfloat16)
    grad_in = contract_rows(first_act, hidden_cot)
    input_cot = contract_cols(hidden_cot, weight_in)
    grad_input = (upstream.astype(jnp.float32) + pull_in(input_cot)[0]).astype(jnp.bfloat16)
    return (grad_input, grad_in, grad_conv, grad_out)


def local(
    embedded,
    mask_token_embedding,
    destination,
    position,
    length,
    unmask_order,
    timestep,
    upstream,
    gain_in,
    weight_in,
    gain_mid,
    weight_conv,
    gain_out,
    weight_out,
):
    channels = embedded.shape[1]
    owners = lax.axis_size("dp")
    own_rows = upstream.shape[0]
    masked_input = jnp.where(
        (unmask_order < timestep)[:, None], mask_token_embedding[None, :], embedded
    )
    row_live = destination < owners
    send_slot = jnp.where(row_live, destination * LMAX + position, owners * LMAX)
    send_rows = (
        jnp.zeros((owners * LMAX + 1, channels), jnp.bfloat16)
        .at[send_slot]
        .set(masked_input)[:-1]
        .reshape(owners, LMAX, channels)
    )
    send_pos = (
        jnp.zeros((owners * LMAX + 1,), jnp.int32)
        .at[send_slot]
        .set(position)[:-1]
        .reshape(owners, LMAX)
    )
    send_len = (
        jnp.zeros((owners * LMAX + 1,), jnp.int32)
        .at[send_slot]
        .set(length)[:-1]
        .reshape(owners, LMAX)
    )
    got_rows, got_pos, got_len = (
        lax.all_to_all(send_rows, "dp", split_axis=0, concat_axis=0, tiled=True),
        lax.all_to_all(send_pos, "dp", split_axis=0, concat_axis=0, tiled=True),
        lax.all_to_all(send_len, "dp", split_axis=0, concat_axis=0, tiled=True),
    )
    slot_used = (got_len.reshape(-1) > 0).astype(jnp.int32)
    target = jnp.where(slot_used > 0, jnp.cumsum(slot_used) - slot_used, own_rows)
    bucket = (
        jnp.zeros((own_rows + 1, channels), jnp.bfloat16)
        .at[target]
        .set(got_rows.reshape(-1, channels))[:own_rows]
    )
    bucket_pos = (
        jnp.zeros((own_rows + 1,), jnp.int32).at[target].set(got_pos.reshape(-1))[:own_rows]
    )
    bucket_len = (
        jnp.zeros((own_rows + 1,), jnp.int32).at[target].set(got_len.reshape(-1))[:own_rows]
    )
    grad_input, grad_in, grad_conv, grad_out = layer_grads(
        bucket,
        upstream,
        bucket_pos,
        bucket_len,
        gain_in,
        weight_in,
        gain_mid,
        weight_conv,
        gain_out,
        weight_out,
    )
    terms = (grad_in[:, None, :], grad_conv, grad_out[:, None, :])
    partial_sums = (
        lax.psum_scatter(terms[0], "shard", scatter_dimension=2, tiled=True),
        lax.psum_scatter(terms[1], "shard", scatter_dimension=2, tiled=True),
        lax.psum_scatter(terms[2], "shard", scatter_dimension=2, tiled=True),
    )
    reduced = (
        lax.psum_scatter(partial_sums[0], "dp", scatter_dimension=0, tiled=True),
        lax.psum_scatter(partial_sums[1], "dp", scatter_dimension=0, tiled=True),
        lax.psum_scatter(partial_sums[2], "dp", scatter_dimension=0, tiled=True),
    )
    reduced_in = reduced[0].reshape(reduced[0].shape[0], reduced[0].shape[2])
    reduced_out = reduced[2].reshape(reduced[2].shape[0], reduced[2].shape[2])
    return (grad_input, reduced_in, reduced[1], reduced_out)


def solution(mesh):
    return jax.shard_map(
        local,
        mesh=mesh,
        in_specs=(
            P(("dp", "shard"), None),
            P(),
            P(("dp", "shard")),
            P(("dp", "shard")),
            P(("dp", "shard")),
            P(("dp", "shard")),
            P(("dp", "shard")),
            P(("dp", "shard"), None),
            P(),
            P(),
            P(),
            P(),
            P(),
            P(),
        ),
        out_specs=(
            P(("dp", "shard"), None),
            P("dp", "shard"),
            P("dp", None, "shard"),
            P("dp", "shard"),
        ),
        check_vma=False,
    )
```

profile of v0, /device:TPU:0, one launch (start us, length us, event | category | flops | bytes accessed | tf_op | source)
XLA Modules:
  0.0 541.9 jit_solution(15636632083457632223)
XLA Ops:
  7.2 0.8 compare_select_fusion.1
  8.0 5.4 scatter_custom_fusion.3
  13.4 0.7 all_to_all.18
  14.1 7.3 %all-to-all-start.2 = ((s32[8,1,80]{2,1,0:T(1,128)}), s32[8,1,80]{2,1,0:T(1,128)S(1)}, u32[]{:S(2)}, u32[]{:S(2)}) async-start(s32[8,1,80]{2,1,0:T(1,128)} %all_to_all.18), calls=%async_computation.2 | async-start | bytes 8192 | tf_op jit(solution)/shard_map/all_to_all | solution.py:154
  21.4 5.4 scatter_custom_fusion
  26.8 0.7 all_to_all.15
  27.8 5.7 %all-to-all-start = ((s32[8,1,80]{2,1,0:T(1,128)}), s32[8,1,80]{2,1,0:T(1,128)S(1)}, u32[]{:S(2)}, u32[]{:S(2)}) async-start(s32[8,1,80]{2,1,0:T(1,128)} %all_to_all.15), calls=%async_computation | async-start | bytes 8192 | tf_op jit(solution)/shard_map/all_to_all | solution.py:155
  33.5 0.7 lt.45
  34.2 10.6 %scatter_custom_fusion.1 = bf16[641,1280]{1,0:T(8,128)(2,1)S(1)} fusion(s32[960]{0:T(1024)S(1)} %compare_select_fusion.1, bf16[960,1280]{1,0:T(8,128)(2,1)} %param.14, pred[960]{0:T(1024)(128)(4,1)S(1)} %lt.45, bf16[1280]{0:T(1024)(128)(2,1)} %param.15, bf16[]{:T(256)} %constant.47.clone.1), kind=kCustom, calls=%fused_computation.18 | custom fusion | flops 1228800 | bytes 4102146 | tf_op jit(solution)/shard_map/scatter | solution.py:137
  44.8 1.3 slice.90
  46.1 6.0 %all-to-all-start.1 = ((bf16[8,80,1280]{2,1,0:T(8,128)(2,1)}), bf16[8,80,1280]{2,1,0:T(8,128)(2,1)S(1)}, u32[]{:S(2)}, u32[]{:S(2)}) async-start(bf16[8,80,1280]{2,1,0:T(8,128)(2,1)} %bitcast.103), calls=%async_computation.1 | async-start | bytes 3276800 | tf_op jit(solution)/shard_map/all_to_all | solution.py:153
  52.7 0.7 reduce.19
  53.8 0.7 fusion.103
  55.0 4.1 scatter_custom_fusion.5
  59.1 4.6 scatter_custom_fusion.4
  63.8 25.8 %all-to-all-done.1 = bf16[8,80,1280]{2,1,0:T(8,128)(2,1)S(1)} async-done(((bf16[8,80,1280]{2,1,0:T(8,128)(2,1)}), bf16[8,80,1280]{2,1,0:T(8,128)(2,1)S(1)}, u32[]{:S(2)}, u32[]{:S(2)}) %all-to-all-start.1) | async-done | bytes 1638432 | tf_op jit(solution)/shard_map/all_to_all | solution.py:153
  89.5 1.2 copy-done.14
  90.7 6.9 %scatter_custom_fusion.2 = bf16[385,1280]{1,0:T(8,128)(2,1)S(1)} fusion(s32[640]{0:T(1024)S(1)} %fusion.77, bf16[640,1280]{1,0:T(8,128)(2,1)} %bitcast.104, bf16[]{:T(256)} %constant.47.clone.1), kind=kCustom, calls=%fused_computation.139 | custom fusion | bytes 986112 | tf_op jit(solution)/shard_map/scatter | solution.py:162
  98.3 5.9 %fusion.13 = (bf16[384,1280]{1,0:T(8,128)(2,1)S(1)}, f32[384,1280]{1,0:T(8,128)}) fusion(f32[1280]{0:T(1024)S(1)} %copy-done.18, f32[384]{0:T(512)S(1)} %fusion.82, f32[384]{0:T(512)S(1)} %broadcast_multiply_fusion.2, bf16[385,1280]{1,0:T(8,128)(2,1)S(1)} %scatter_custom_fusion.2), kind=kLoop, calls=%fused_computation.27 | loop fusion | flops 33914880 | bytes 3940352 | tf_op jit(solution)/shard_map/convert_element_type | solution.py:57
  104.2 1.0 fusion.110
  105.5 2.9 multiply_convert_fusion.1
  108.6 0.6 fusion.59
  109.3 0.7 convolution_add_fusion.3
  110.0 0.7 convolution_add_fusion.2
  110.7 0.7 convolution_add_fusion.1
  111.4 0.8 fusion.111
  112.6 0.6 copy-done.20
  113.1 3.3 multiply_reduce_fusion.1
  116.4 1.0 fusion.105
  117.5 0.6 fusion.46
  118.2 0.6 fusion.49
  118.8 0.6 fusion.54
  119.4 0.6 fusion.57
  120.4 3.4 multiply_reduce_fusion
  124.3 0.9 copy-done.15
  125.2 2.9 convolution_bitcast_fusion.1
  128.1 7.8 %copy.23 = f32[1280,1,640]{0,1,2:T(1,128)} copy(f32[1280,1,640]{2,0,1:T(8,128)} %convolution_bitcast_fusion.1) | data formatting | bytes 6553600 | tf_op jit(solution)/shard_map/broadcast_in_dim | solution.py:182
  136.0 4.7 convolution_bitcast_fusion
  140.8 3.0 bitcast_dynamic-update-slice_fusion.4
  143.8 2.0 bitcast_dynamic-update-slice_fusion.3
  145.8 1.9 bitcast_dynamic-update-slice_fusion.2
  147.7 2.0 bitcast_dynamic-update-slice_fusion.1
  149.7 2.0 bitcast_dynamic-update-slice_fusion
  151.6 13.4 %copy.29 = f32[640,5,640]{0,1,2:T(8,128)} copy(f32[640,5,640]{2,0,1:T(8,128)} %bitcast_dynamic-update-slice_fusion) | data formatting | bytes 16384000
  165.1 9.9 %copy.37 = f32[80,8,5,640]{3,1,2,0:T(8,128)} copy(f32[80,8,5,640]{3,2,1,0:T(8,128)} %bitcast.100) | data formatting | bytes 16384000
  175.1 0.6 copy-done.21
  175.6 0.6 dynamic-slice
  176.9 28.6 %all-reduce.11.cloned.1.call-done = f32[1280,1,640]{0,1,2:T(1,128)} async-done(((f32[1280,1,640]{0,1,2:T(1,128)}), f32[1280,1,640]{0,1,2:T(1,128)}) %all-reduce.11.cloned.1.call-update) | async-done | bytes 3276816
  205.5 1.7 constant_dynamic-slice_fusion
  207.2 48.3 %copy.27 = f32[1280,1,160]{1,2,0:T(8,128)} copy(f32[1280,1,160]{0,1,2:T(1,128)S(1)} %constant_dynamic-slice_fusion) | data formatting | bytes 1638400
  255.5 50.9 %bitcast_reduce_fusion = f32[1280,160]{1,0:T(8,128)} fusion(f32[1280,1,160]{1,2,0:T(8,128)} %copy.27), kind=kLoop, calls=%fused_computation.6 | loop fusion | bytes 1638400
  306.8 2.6 copy.34
  309.5 10.3 %reduce-scatter.18.cloned.1.call-done = f32[160,3200]{1,0:T(8,128)} async-done(((f32[640,3200]{1,0:T(8,128)}), f32[160,3200]{1,0:T(8,128)}) %reduce-scatter.18.cloned.1.call-update) | async-done | bytes 2048016
  319.8 3.6 reshape.254
  323.4 4.6 copy.30
  328.0 3.5 fusion.21
  331.6 0.6 fusion.102
  332.2 0.6 copy-done.12
  332.7 1.6 add_convert_fusion
  334.4 53.7 %reduce-scatter.16.cloned.1.call-done = f32[160,160]{1,0:T(8,128)} async-done(((f32[1280,160]{1,0:T(8,128)}), f32[160,160]{1,0:T(8,128)}) %reduce-scatter.16.cloned.1.call-update) | async-done | bytes 102416
  388.1 8.4 %reshape_bitcast_fusion = f32[160,1,160]{1,2,0:T(8,128)} fusion(f32[160,160]{1,0:T(8,128)} %reduce-scatter.16.cloned.1.call-done), kind=kLoop, calls=%fused_computation.7 | loop fusion | bytes 204800
  396.5 9.6 %copy.26 = f32[160,1,160]{2,0,1:T(8,128)} copy(f32[160,1,160]{1,2,0:T(8,128)} %reshape_bitcast_fusion) | data formatting | bytes 204800
  406.1 49.8 %reduce-scatter.20.cloned.1.call-done = f32[160,160]{1,0:T(8,128)} async-done(((f32[1280,160]{1,0:T(8,128)}), f32[160,160]{1,0:T(8,128)}) %reduce-scatter.20.cloned.1.call-update) | async-done | bytes 102416
  455.9 78.7 %reduce-scatter.12.cloned.1.call-done = f32[80,5,160]{2,0,1:T(8,128)} async-done(((f32[640,5,160]{2,0,1:T(8,128)}), f32[80,5,160]{2,0,1:T(8,128)}) %reduce-scatter.12.cloned.1.call-update) | async-done | bytes 256016 | tf_op jit(solution)/shard_map/reduce_scatter | solution.py:190
  (91 shorter events, 5.1 us)
Async XLA Ops:
  7.2 97.0 %copy-start = (bf16[1280,640]{1,0:T(8,128)(2,1)S(1)}, bf16[1280,640]{1,0:T(8,128)(2,1)}, u32[]{:S(2)}) copy-start(bf16[1280,640]{1,0:T(8,128)(2,1)} %param.23) | copy-start | bytes 4915204
  14.1 13.7 %all-to-all-start.2 = ((s32[8,1,80]{2,1,0:T(1,128)}), s32[8,1,80]{2,1,0:T(1,128)S(1)}, u32[]{:S(2)}, u32[]{:S(2)}) async-start(s32[8,1,80]{2,1,0:T(1,128)} %all_to_all.18), calls=%async_computation.2 | async-start | bytes 8192 | tf_op jit(solution)/shard_map/all_to_all | solution.py:154
  27.8 18.3 %all-to-all-start = ((s32[8,1,80]{2,1,0:T(1,128)}), s32[8,1,80]{2,1,0:T(1,128)S(1)}, u32[]{:S(2)}, u32[]{:S(2)}) async-start(s32[8,1,80]{2,1,0:T(1,128)} %all_to_all.15), calls=%async_computation | async-start | bytes 8192 | tf_op jit(solution)/shard_map/all_to_all | solution.py:155
  46.1 43.4 %all-to-all-start.1 = ((bf16[8,80,1280]{2,1,0:T(8,128)(2,1)}), bf16[8,80,1280]{2,1,0:T(8,128)(2,1)S(1)}, u32[]{:S(2)}, u32[]{:S(2)}) async-start(bf16[8,80,1280]{2,1,0:T(8,128)(2,1)} %bitcast.103), calls=%async_computation.1 | async-start | bytes 3276800 | tf_op jit(solution)/shard_map/all_to_all | solution.py:153
  52.1 46.1 %copy-start.18 = (f32[1280]{0:T(1024)S(1)}, f32[1280]{0:T(1024)}, u32[]{:S(2)}) copy-start(f32[1280]{0:T(1024)} %param.22) | copy-start | bytes 15364
  52.1 153.4 %all-reduce.11.cloned.1.call-start = ((), (), s32[]{:S(2)}) async-start(), calls=%async_computation.13 | async-start | bytes 6553600
  89.5 1.2 copy-start.14
  104.2 1.3 copy-start.19
  105.5 3.1 copy-start.4
  108.4 1.6 copy-start.1
  108.5 0.8 copy-start.16
  108.5 2.9 copy-start.9
  108.6 1.4 copy-start.7
  108.6 2.1 copy-start.5
  111.4 1.2 copy-start.11
  111.4 1.2 copy-start.17
  111.4 1.7 copy-start.20
  112.2 4.3 copy-start.3
  116.4 1.0 copy-start.13
  124.3 1.0 copy-start.15
  135.9 170.9 %reduce-scatter.14.cloned.1.call-start = ((), (), s32[]{:S(2)}) async-start(), calls=%async_computation.9 | async-start | bytes 4096000 | tf_op jit(solution)/shard_map/reduce_scatter | solution.py:186
  140.7 179.1 %reduce-scatter.18.cloned.1.call-start = ((), (), s32[]{:S(2)}) async-start(), calls=%async_computation.11 | async-start | bytes 10240000
  140.7 3.0 copy-start.8
  143.8 2.0 copy-start.2
  143.8 3.9 copy-start.6
  145.8 3.9 copy-start.10
  175.0 0.7 copy-start.21
  175.0 213.1 %reduce-scatter.16.cloned.1.call-start = ((), (), s32[]{:S(2)}) async-start(), calls=%async_computation.10 | async-start | bytes 1474560
  306.4 149.4 %reduce-scatter.20.cloned.1.call-start = ((), (), s32[]{:S(2)}) async-start(), calls=%async_computation.12 | async-start | bytes 1474560
  309.4 225.2 %reduce-scatter.12.cloned.1.call-start = ((), (), s32[]{:S(2)}) async-start(), calls=%async_computation.8 | async-start | bytes 3686400 | tf_op jit(solution)/shard_map/reduce_scatter | solution.py:190
  331.5 1.2 copy-start.12
Sparse Core Ops, SparseCore 0:
  136.0 69.4 all-reduce.10
  208.1 38.8 reduce-scatter.13
  249.6 70.1 reduce-scatter.17
  323.1 64.9 reduce-scatter.15
  391.9 63.9 reduce-scatter.19
  459.9 74.6 reduce-scatter.11
where the time goes:
time: 552 us; the launch traced here: 542 us
  waiting for transfers between devices  247 us (45%)
  local copies, waits for them, and re-layouts  196 us (36%)
  matrix products  35.5 us (6%)
  other arithmetic  28 us (5%)
  starting transfers between devices  19.5 us (4%)
  between operations  15.7 us (3%)
    unnamed x55, local copies, waits for them, and re-layouts  158 us
    unnamed x10, waiting for transfers between devices  143 us
    reduce_scatter x1, waiting for transfers between devices, local(): lax.psum_scatter(partial_sums[1], 'dp', scatter_dimension=0, tiled=True)  78.7 us
    all_to_all x1, waiting for transfers between devices, local(): lax.all_to_all(send_rows, 'dp', split_axis=0, concat_axis=0, tiled=True)  25.8 us
    dot_general x7, matrix products, contract_rows(): lax.dot_general(left, right, (((0,), (0,)), ((), ())), preferred_element_...  18.5 us
  transfers between devices with their start and end apart: 9, of which 7 were waited for; matrix products, arithmetic and copies ran while one was open for 38% of the time, Pallas kernels for 0%

commit v1 on v0

--- a/solution.py
+++ b/solution.py
@@ -1,6 +1,9 @@
 import jax
 import jax.numpy as jnp
 from jax import lax
+from jax.experimental import pallas as pl
+from jax.experimental.pallas import tpu as pltpu
+import functools
 from jax.sharding import PartitionSpec as P
 
 KERNEL_TAPS = 5
@@ -83,16 +86,8 @@
         )
     out_f32, pull_out = jax.vjp(lambda value: normalized_activation(value, gain_out), conv)
     out_act = out_f32.astype(jnp.bfloat16)
-    grad_out = contract_rows(upstream, out_act)
     out_cot = jnp.dot(upstream, weight_out, preferred_element_type=jnp.float32)
     conv_cot = pull_out(out_cot)[0].astype(jnp.bfloat16)
-    grad_conv = jnp.stack(
-        [
-            contract_rows(tap_list[kernel_tap_index], conv_cot)
-            for kernel_tap_index in range(KERNEL_TAPS)
-        ],
-        axis=1,
-    )
     mid_cot = jnp.zeros(mid_act.shape, jnp.float32)
     for kernel_tap_index in range(KERNEL_TAPS):
         back_term = contract_cols(conv_cot, weight_conv[:, kernel_tap_index, :])
@@ -101,10 +96,174 @@
         )
         mid_cot = mid_cot + raw_shift(back_term, -tap_offsets[kernel_tap_index])
     hidden_cot = pull_mid(mid_cot)[0].astype(jnp.bfloat16)
-    grad_in = contract_rows(first_act, hidden_cot)
     input_cot = contract_cols(hidden_cot, weight_in)
     grad_input = (upstream.astype(jnp.float32) + pull_in(input_cot)[0]).astype(jnp.bfloat16)
-    return (grad_input, grad_in, grad_conv, grad_out)
+    return (grad_input, first_act, mid_act, out_act, conv_cot, hidden_cot)
+
+
+MESH = pl.DeviceIdType.MESH
+
+
+def bit_orders(owners, groups):
+    dp_bits = [("dp", i) for i in range(owners.bit_length() - 1)]
+    sh_bits = [("shard", i) for i in range(groups.bit_length() - 1)]
+    first, others = sh_bits[:1], sh_bits[1:]
+    return (
+        first + others + dp_bits,
+        first + dp_bits[:1] + others + dp_bits[1:],
+        first + dp_bits[1:] + others + dp_bits[:1],
+    )
+
+
+def place(order, owner, group):
+    index = 0
+    for axis, bit in order:
+        index = index * 2 + (((owner if axis == "dp" else group) >> bit) & 1)
+    return index
+
+
+def chunk_rows(rows):
+    unit = rows // 5
+    return (2 * unit, 2 * unit, unit)
+
+
+def round_up(value, multiple):
+    return -(-value // multiple) * multiple
+
+
+def placed(values, offset):
+    low = offset // 128 * 128
+    high = round_up(offset + values.shape[1], 128)
+    parts = []
+    if offset > low:
+        parts.append(jnp.zeros((values.shape[0], offset - low), values.dtype))
+    parts.append(values)
+    if high > offset + values.shape[1]:
+        parts.append(jnp.zeros((values.shape[0], high - offset - values.shape[1]), values.dtype))
+    return low, (jnp.concatenate(parts, axis=1) if len(parts) > 1 else values)
+
+
+def weight_terms_kernel(
+    owners, groups, position, length, mid, conv_cot, first, hidden_cot, upstream, out_act, *outs
+):
+    taps = []
+    for k in range(KERNEL_TAPS):
+        offset = (k - KERNEL_TAPS // 2) * DILATION_STEP
+        moved = position[...] + offset
+        valid = (moved >= 0) & (moved < length[...])
+        shifted = raw_shift(mid[...], offset).astype(jnp.float32)
+        taps.append(jnp.where(valid, shifted, 0.0))
+    narrow, wide = mid.shape[1] // owners, first.shape[1] // owners
+    rows = conv_cot.shape[1] // groups
+    width = outs[0].shape[2]
+    conv_t, hidden_t, out_t = conv_cot[...].T, hidden_cot[...].T, out_act[...].T
+    orders = bit_orders(owners, groups)
+    for owner in range(owners):
+        here = slice(owner * narrow, (owner + 1) * narrow)
+        there = slice(owner * wide, (owner + 1) * wide)
+        left = (
+            (conv_t, jnp.concatenate([t[:, here] for t in taps], axis=1), 0),
+            (hidden_t, first[:, there].astype(jnp.float32), KERNEL_TAPS * narrow),
+            (out_t, upstream[:, there].astype(jnp.float32), KERNEL_TAPS * narrow + wide),
+        )
+        tiles = [None] * (width // 128)
+        for right, values, offset in left:
+            low, padded = placed(values, offset)
+            term = jnp.dot(
+                right, padded.astype(jnp.bfloat16), preferred_element_type=jnp.float32
+            )
+            for j in range(padded.shape[1] // 128):
+                piece = term[:, j * 128 : (j + 1) * 128]
+                at = low // 128 + j
+                tiles[at] = piece if tiles[at] is None else tiles[at] + piece
+        for j, tile in enumerate(tiles):
+            tile = tile.astype(jnp.bfloat16)
+            for group in range(groups):
+                start = group * rows
+                for order, out, count in zip(orders, outs, chunk_rows(rows)):
+                    out[place(order, owner, group), :, j * 128 : (j + 1) * 128] = tile[
+                        start : start + count
+                    ]
+                    start += count
+
+
+def reduce_kernel(owners, groups, *refs):
+    chunks = 3
+    terms, outs = refs[:chunks], refs[chunks : 2 * chunks]
+    got, sums = refs[2 * chunks : 3 * chunks], refs[3 * chunks : 4 * chunks]
+    send_sem, recv_sem = refs[4 * chunks :]
+    orders = bit_orders(owners, groups)
+    steps = len(orders[0])
+    me = {"dp": lax.axis_index("dp"), "shard": lax.axis_index("shard")}
+
+    def bit_of(axis, bit):
+        return lax.rem(me[axis] // (1 << bit), 2)
+
+    def partner(axis, bit):
+        other = me[axis] + (1 - 2 * bit_of(axis, bit)) * (1 << bit)
+        return (other, me["shard"]) if axis == "dp" else (me["dp"], other)
+
+    barrier = pltpu.get_barrier_semaphore()
+    for axis, bit in orders[0]:
+        pl.semaphore_signal(barrier, inc=1, device_id=partner(axis, bit), device_id_type=MESH)
+    pl.semaphore_wait(barrier, steps)
+
+    total = 1 << steps
+    base, at = [], 0
+    for t in range(steps):
+        base.append(at)
+        at += total >> (t + 1)
+
+    def copy_of(c, t):
+        half = total >> (t + 1)
+        away = 1 - bit_of(*orders[c][t])
+        source = terms[c] if t == 0 else sums[c]
+        start = away * half if t == 0 else base[t - 1] + away * half
+        return pltpu.make_async_remote_copy(
+            src_ref=source.at[pl.ds(start, half)],
+            dst_ref=got[c].at[pl.ds(base[t], half)],
+            send_sem=send_sem.at[c, t],
+            recv_sem=recv_sem.at[c, t],
+            device_id=partner(*orders[c][t]),
+            device_id_type=MESH,
+        )
+
+    def add(c, t, first, count):
+        half = total >> (t + 1)
+        kept = bit_of(*orders[c][t]) * half
+        source = terms[c] if t == 0 else sums[c]
+        offset = kept if t == 0 else base[t - 1] + kept
+
+        def body(i, carry):
+            at = first + i
+            value = source[offset + at].astype(jnp.float32) + got[c][base[t] + at].astype(
+                jnp.float32
+            )
+            if t == steps - 1:
+                outs[c][...] = value
+            else:
+                sums[c][base[t] + at] = value.astype(jnp.bfloat16)
+            return carry
+
+        lax.fori_loop(0, count, body, 0)
+
+    copies = [[copy_of(c, t) for t in range(steps)] for c in range(chunks)]
+    for c in range(chunks):
+        copies[c][0].start()
+    for t in range(steps):
+        for c in range(chunks):
+            copies[c][t].wait_recv()
+            half = total >> (t + 1)
+            if t == steps - 1:
+                add(c, t, 0, 1)
+            else:
+                nxt = bit_of(*orders[c][t + 1])
+                add(c, t, (1 - nxt) * (half // 2), half // 2)
+                copies[c][t + 1].start()
+                add(c, t, nxt * (half // 2), half // 2)
+    for c in range(chunks):
+        for t in range(steps):
+            copies[c][t].wait_send()
 
 
 def local(
@@ -124,50 +283,49 @@
     weight_out,
 ):
     channels = embedded.shape[1]
-    owners = lax.axis_size("dp")
+    owners, groups = lax.axis_size("dp"), lax.axis_size("shard")
     own_rows = upstream.shape[0]
+    inner = weight_in.shape[1]
     masked_input = jnp.where(
         (unmask_order < timestep)[:, None], mask_token_embedding[None, :], embedded
     )
-    row_live = destination < owners
-    send_slot = jnp.where(row_live, destination * LMAX + position, owners * LMAX)
-    send_rows = (
-        jnp.zeros((owners * LMAX + 1, channels), jnp.bfloat16)
-        .at[send_slot]
-        .set(masked_input)[:-1]
-        .reshape(owners, LMAX, channels)
-    )
-    send_pos = (
-        jnp.zeros((owners * LMAX + 1,), jnp.int32)
-        .at[send_slot]
-        .set(position)[:-1]
-        .reshape(owners, LMAX)
-    )
-    send_len = (
-        jnp.zeros((owners * LMAX + 1,), jnp.int32)
-        .at[send_slot]
-        .set(length)[:-1]
-        .reshape(owners, LMAX)
-    )
-    got_rows, got_pos, got_len = (
-        lax.all_to_all(send_rows, "dp", split_axis=0, concat_axis=0, tiled=True),
-        lax.all_to_all(send_pos, "dp", split_axis=0, concat_axis=0, tiled=True),
-        lax.all_to_all(send_len, "dp", split_axis=0, concat_axis=0, tiled=True),
-    )
-    slot_used = (got_len.reshape(-1) > 0).astype(jnp.int32)
-    target = jnp.where(slot_used > 0, jnp.cumsum(slot_used) - slot_used, own_rows)
-    bucket = (
-        jnp.zeros((own_rows + 1, channels), jnp.bfloat16)
-        .at[target]
-        .set(got_rows.reshape(-1, channels))[:own_rows]
-    )
-    bucket_pos = (
-        jnp.zeros((own_rows + 1,), jnp.int32).at[target].set(got_pos.reshape(-1))[:own_rows]
-    )
-    bucket_len = (
-        jnp.zeros((own_rows + 1,), jnp.int32).at[target].set(got_len.reshape(-1))[:own_rows]
-    )
-    grad_input, grad_in, grad_conv, grad_out = layer_grads(
+    depth = LMAX + 8
+    slot = jnp.where(destination < owners, destination * depth + position, -1)
+    pick = (jnp.arange(owners * depth, dtype=jnp.int32)[:, None] == slot[None, :]).astype(
+        jnp.bfloat16
+    )
+    send_len = jnp.max(
+        jnp.where(
+            destination[None, :] == jnp.arange(owners, dtype=jnp.int32)[:, None],
+            length[None, :],
+            0,
+        ),
+        axis=1,
+    )
+    send = jnp.dot(pick, masked_input, preferred_element_type=jnp.float32)
+    send = send.reshape(owners, depth, channels)
+    in_block = jnp.arange(depth, dtype=jnp.int32)[None, :, None]
+    send = jnp.where(
+        in_block >= LMAX, send_len[:, None, None].astype(jnp.float32), send
+    ).astype(jnp.bfloat16)
+    got = lax.all_to_all(send, "dp", split_axis=0, concat_axis=0, tiled=True)
+    got_len = got[:, LMAX, 0].astype(jnp.int32)
+    ends = jnp.cumsum(got_len)
+    starts = ends - got_len
+    row = jnp.arange(own_rows, dtype=jnp.int32)
+    mine = (row[:, None] >= starts[None, :]) & (row[:, None] < ends[None, :])
+    bucket_pos = jnp.sum(jnp.where(mine, row[:, None] - starts[None, :], 0), axis=1)
+    bucket_len = jnp.sum(jnp.where(mine, got_len[None, :], 0), axis=1)
+    source = jnp.sum(
+        jnp.where(mine, jnp.arange(owners, dtype=jnp.int32)[None, :] * depth, 0), axis=1
+    )
+    take = (
+        (source + bucket_pos)[:, None] == jnp.arange(owners * depth, dtype=jnp.int32)[None, :]
+    ).astype(jnp.bfloat16)
+    bucket = jnp.dot(
+        take, got.reshape(-1, channels), preferred_element_type=jnp.float32
+    ).astype(jnp.bfloat16)
+    grad_input, first_act, mid_act, out_act, conv_cot, hidden_cot = layer_grads(
         bucket,
         upstream,
         bucket_pos,
@@ -179,20 +337,46 @@
         gain_out,
         weight_out,
     )
-    terms = (grad_in[:, None, :], grad_conv, grad_out[:, None, :])
-    partial_sums = (
-        lax.psum_scatter(terms[0], "shard", scatter_dimension=2, tiled=True),
-        lax.psum_scatter(terms[1], "shard", scatter_dimension=2, tiled=True),
-        lax.psum_scatter(terms[2], "shard", scatter_dimension=2, tiled=True),
-    )
-    reduced = (
-        lax.psum_scatter(partial_sums[0], "dp", scatter_dimension=0, tiled=True),
-        lax.psum_scatter(partial_sums[1], "dp", scatter_dimension=0, tiled=True),
-        lax.psum_scatter(partial_sums[2], "dp", scatter_dimension=0, tiled=True),
-    )
-    reduced_in = reduced[0].reshape(reduced[0].shape[0], reduced[0].shape[2])
-    reduced_out = reduced[2].reshape(reduced[2].shape[0], reduced[2].shape[2])
-    return (grad_input, reduced_in, reduced[1], reduced_out)
+    narrow, wide, rows = inner // owners, channels // owners, inner // groups
+    width = round_up(KERNEL_TAPS * narrow + 2 * wide, 128)
+    total = owners * groups
+    vmem = pl.BlockSpec(memory_space=pltpu.VMEM)
+    counts = chunk_rows(rows)
+    terms = pl.pallas_call(
+        functools.partial(weight_terms_kernel, owners, groups),
+        out_shape=[jax.ShapeDtypeStruct((total, n, width), jnp.bfloat16) for n in counts],
+        in_specs=[vmem] * 8,
+        out_specs=[vmem] * 3,
+        compiler_params=pltpu.CompilerParams(vmem_limit_bytes=60 * 1024 * 1024),
+        name="weight_terms",
+    )(
+        bucket_pos[:, None],
+        bucket_len[:, None],
+        mid_act,
+        conv_cot,
+        first_act,
+        hidden_cot,
+        upstream,
+        out_act,
+    )
+    steps = total.bit_length() - 1
+    reduced = pl.pallas_call(
+        functools.partial(reduce_kernel, owners, groups),
+        out_shape=[jax.ShapeDtypeStruct((n, width), jnp.float32) for n in counts],
+        in_specs=[vmem] * 3,
+        out_specs=[vmem] * 3,
+        scratch_shapes=[pltpu.VMEM((total - 1, n, width), jnp.bfloat16) for n in counts]
+        + [pltpu.VMEM((total - 1, n, width), jnp.bfloat16) for n in counts]
+        + [pltpu.SemaphoreType.DMA((3, steps)), pltpu.SemaphoreType.DMA((3, steps))],
+        compiler_params=pltpu.CompilerParams(
+            collective_id=0, has_side_effects=True, vmem_limit_bytes=60 * 1024 * 1024
+        ),
+        name="reduce_terms",
+    )(*terms)
+    reduced = jnp.concatenate(reduced, axis=0).T
+    cut = KERNEL_TAPS * narrow
+    reduced_conv = reduced[:cut].reshape(KERNEL_TAPS, narrow, rows).transpose(1, 0, 2)
+    return (grad_input, reduced[cut : cut + wide], reduced_conv, reduced[cut + wide : cut + 2 * wide])
 
 
 def solution(mesh):

time: 552 us -> 171 us (0.31); the launches traced: 542 us -> 169 us
  waiting for transfers between devices: 247 us -> 41.9 us
  local copies, waits for them, and re-layouts: 196 us -> 6.65 us
  Pallas kernels: 0 us -> 67.2 us
  matrix products: 35.5 us -> 19 us
  between operations: 15.7 us -> 1.02 us
  starting transfers between devices: 19.5 us -> 7.31 us
    unnamed x55 -> x32, local copies, waits for them, and re-layouts: 158 us -> 2.96 us
    unnamed x10 -> x0, waiting for transfers between devices: 143 us -> none
    reduce_scatter x2 -> x0, waiting for transfers between devices: 78.7 us -> none  [the longest x1 78.7 us: local(): lax.psum_scatter(partial_sums[1], 'dp', scatter_dimension=0, tiled=True)]
    pallas_call x0 -> x2, Pallas kernels: none -> 67.2 us  [the longest x1 55.1 us: local(): pl.pallas_call(functools.partial(reduce_kernel, owners, groups), out_shap...]
    scatter x5 -> x0, local copies, waits for them, and re-layouts: 26.4 us -> none  [the longest x1 6.9 us: local(): bucket = jnp.zeros((own_rows + 1, channels), jnp.bfloat16).at[target].set...]
    all_to_all x3 -> x1, waiting for transfers between devices: 26.1 us -> 41.9 us  [local(): got = lax.all_to_all(send, 'dp', split_axis=0, concat_axis=0, tiled=True)]
    dot_general x7 -> x2, matrix products: 18.5 us -> 5.07 us  [the longest x1 3.99 us: local(): send = jnp.dot(pick, masked_input, preferred_element_type=jnp.float32)]
    all_to_all x3 -> x1, starting transfers between devices: 19 us -> 7.31 us  [local(): got = lax.all_to_all(send, 'dp', split_axis=0, concat_axis=0, tiled=True)]
  transfers between devices with their start and end apart: 9 -> 1, of which waited for: 7 -> 1; matrix products, arithmetic and copies ran while one was open for 38% -> 0% of each run, Pallas kernels for 0% -> 0%
where the time goes in v1:
time: 171 us; the launch traced here: 169 us
  Pallas kernels  67.2 us (39%)
  waiting for transfers between devices  41.9 us (25%)
  other arithmetic  25.8 us (15%)
  matrix products  19 us (11%)
  starting transfers between devices  7.31 us (4%)
  local copies, waits for them, and re-layouts  6.65 us (4%)
    pallas_call x1, Pallas kernels, local(): pl.pallas_call(functools.partial(reduce_kernel, owners, groups), out_shap...  55.1 us
    all_to_all x1, waiting for transfers between devices, local(): got = lax.all_to_all(send, 'dp', split_axis=0, concat_axis=0, tiled=True)  41.9 us
    pallas_call x1, Pallas kernels, local(): pl.pallas_call(functools.partial(weight_terms_kernel, owners, groups), ou...  12.2 us
    dot_general x6, matrix products, contract_cols(): lax.dot_general(left, right, (((1,), (1,)), ((), ())), preferred_element_...  8.25 us
    all_to_all x1, starting transfers between devices, local(): got = lax.all_to_all(send, 'dp', split_axis=0, concat_axis=0, tiled=True)  7.31 us
    convert_element_type x1, other arithmetic, layer_grads(): first_act = first_f32.astype(jnp.bfloat16)  4.91 us
    reduce_sum x3, other arithmetic, normalized_activation(): centred = values - row_mean  4.05 us
    dot_general x1, matrix products, local(): send = jnp.dot(pick, masked_input, preferred_element_type=jnp.float32)  3.99 us
  transfers between devices with their start and end apart: 1, of which 1 were waited for; matrix products, arithmetic and copies ran while one was open for 0% of the time, Pallas kernels for 0%

profile of v1, /device:TPU:0, one launch (start us, length us, event | category | flops | bytes accessed | tf_op | source)
XLA Modules:
  0.0 169.0 jit_solution(7271276664629510345)
XLA Ops:
  0.6 0.0 copy-start
  0.7 0.8 add_select_fusion
  1.5 0.8 select_reduce_fusion
  2.3 0.7 lt.57
  3.0 4.0 %fusion = bf16[704,1280]{1,0:T(8,128)(2,1)S(1)} fusion(bf16[960,1280]{1,0:T(8,128)(2,1)} %param.14, pred[960]{0:T(1024)(128)(4,1)S(1)} %lt.57, s32[960]{0:T(1024)S(1)} %add_select_fusion, bf16[1280]{0:T(1024)(128)(2,1)} %param.15), kind=kOutput, calls=%fused_computation.4 | convolution fusion | flops 1732055040 | bytes 4267200 | tf_op jit(solution)/shard_map/dot_general | solution.py:305
  7.0 1.4 select_convert_fusion
  8.5 7.3 %all-to-all-start = ((bf16[8,88,1280]{2,1,0:T(8,128)(2,1)}), bf16[8,88,1280]{2,1,0:T(8,128)(2,1)S(1)}, u32[]{:S(2)}, u32[]{:S(2)}) async-start(bf16[8,88,1280]{2,1,0:T(8,128)(2,1)} %select_convert_fusion), calls=%async_computation | async-start | bytes 3604480 | tf_op jit(solution)/shard_map/all_to_all | solution.py:311
  15.8 41.9 %all-to-all-done = bf16[8,88,1280]{2,1,0:T(8,128)(2,1)S(1)} async-done(((bf16[8,88,1280]{2,1,0:T(8,128)(2,1)}), bf16[8,88,1280]{2,1,0:T(8,128)(2,1)S(1)}, u32[]{:S(2)}, u32[]{:S(2)}) %all-to-all-start) | async-done | bytes 1802272 | tf_op jit(solution)/shard_map/all_to_all | solution.py:311
  57.7 0.2 fusion.73
  57.9 0.2 reduce-window.7
  58.1 0.1 select_reduce_fusion.1
  58.2 1.1 fusion.90
  59.3 0.0 copy-start.11
  59.3 0.3 multiply_reduce_fusion.1
  59.7 0.3 copy-done.11
  60.0 4.9 %multiply_convert_fusion = (bf16[384,1280]{1,0:T(8,128)(2,1)S(1)}, f32[384,1280]{1,0:T(8,128)S(1)}) fusion(f32[384,1280]{1,0:T(8,128)S(1)} %get-tuple-element.57, f32[1280]{0:T(1024)S(1)} %copy-done.11, f32[384]{0:T(512)S(1)} %fusion.74, f32[384]{0:T(512)S(1)} %broadcast_multiply_fusion.2), kind=kLoop, calls=%fused_computation.13 | loop fusion | flops 33423360 | bytes 4923392 | tf_op jit(solution)/shard_map/convert_element_type | solution.py:60
  65.0 0.0 copy-start.8
  65.0 0.0 copy-done
  65.0 0.0 copy-start.13
  65.0 1.0 fusion.91
  66.0 0.3 multiply_reduce_fusion.5
  66.3 0.0 copy-start.5
  66.3 2.7 %multiply_convert_fusion.2.mid = bf16[384,640]{1,0:T(8,128)(2,1)S(1)} fusion(f32[384,640]{1,0:T(8,128)S(1)} %get-tuple-element.59, f32[640]{0:T(1024)S(1)} %copy-done.13, f32[384]{0:T(512)S(1)} %fusion.75, f32[384]{0:T(512)S(1)} %broadcast_multiply_fusion.1), kind=kLoop, calls=%fused_computation.67 | loop fusion | flops 16711680 | bytes 1480192 | tf_op jit(solution)/shard_map/convert_element_type | solution.py:63
  69.0 0.1 fusion.88
  69.1 0.1 fusion.89
  69.2 0.0 copy-done.5
  69.2 0.6 fusion.40
  69.9 0.7 convolution_add_fusion.3
  70.5 0.7 convolution_add_fusion.2
  71.2 0.6 convolution_add_fusion.1
  71.8 0.0 copy-start.12
  71.8 0.8 fusion.92
  72.6 0.0 copy-start.14
  72.6 0.3 multiply_reduce_fusion.4
  72.9 3.4 %multiply_convert_fusion.1 = (bf16[384,640]{1,0:T(8,128)(2,1)}, f32[384,640]{1,0:T(8,128)S(1)}) fusion(f32[384,640]{1,0:T(8,128)S(1)} %get-tuple-element.61, f32[640]{0:T(1024)S(1)} %copy-done.12, f32[384]{0:T(512)S(1)} %fusion.76, f32[384]{0:T(512)S(1)} %broadcast_multiply_fusion), kind=kLoop, calls=%fused_computation.46 | loop fusion | flops 16711680 | bytes 2463232 | tf_op jit(solution)/shard_map/convert_element_type | solution.py:88
  76.3 1.4 multiply_reduce_fusion.3
  77.7 1.0 fusion.85
  78.6 0.1 add_convert_fusion.2.conv_cot
  78.8 0.6 fusion.27
  79.4 0.6 fusion.38
  80.0 0.1 slice.78
  80.1 0.6 fusion.30
  80.7 0.6 fusion.35
  81.3 0.1 slice.80
  81.4 0.8 reduce_sum.180.position
  82.2 0.8 reduce_sum.181.length
  82.9 0.2 slice_select_fusion.2
  83.2 0.2 slice_select_fusion
  83.4 3.2 %multiply_reduce_fusion.2 = (f32[384]{0:T(512)S(1)}, f32[384,640]{1,0:T(8,128)S(1)}) fusion(f32[384,640]{1,0:T(8,128)S(1)} %get-tuple-element.59, f32[384]{0:T(512)S(1)} %broadcast_multiply_fusion.1, f32[352,640]{1,0:T(8,128)S(1)} %get-tuple-element.70, f32[368,640]{1,0:T(8,128)S(1)} %get-tuple-element.68, ...), kind=kOutput, calls=%fused_computation.48 | convolution fusion | flops 334724736 | bytes 6973440 | tf_op jit(solution)/shard_map/dot_general | solution.py:41
  86.6 0.4 fusion.84
  87.0 0.9 add_convert_fusion.1.hidden_cot
  87.9 12.2 %weight_terms.1 = (bf16[32,64,768]{2,1,0:T(8,128)(2,1)}, bf16[32,64,768]{2,1,0:T(8,128)(2,1)}, bf16[32,32,768]{2,1,0:T(8,128)(2,1)}) custom-call(s32[384,1]{1,0:T(8,128)} %reduce_sum.180.position, s32[384,1]{1,0:T(8,128)} %reduce_sum.181.length, bf16[384,640]{1,0:T(8,128)(2,1)} %copy-done.1, bf16[384,640]{1,0:T(8,128)(2,1)} %copy-done.2, ...), custom_call_target="tpu_custom_call" | custom-call | tf_op jit(solution)/shard_map/weight_terms/pallas_call | solution.py:345
  100.1 55.1 %reduce_terms.1 = (f32[64,768]{1,0:T(8,128)}, f32[64,768]{1,0:T(8,128)}, f32[32,768]{1,0:T(8,128)}) custom-call(bf16[32,64,768]{2,1,0:T(8,128)(2,1)} %get-tuple-element.10.refs_0_, bf16[32,64,768]{2,1,0:T(8,128)(2,1)} %get-tuple-element.11.refs_1_, bf16[32,32,768]{2,1,0:T(8,128)(2,1)} %get-tuple-element.12.refs_2_), custom_call_target="tpu_custom_call" | custom-call | tf_op jit(solution)/shard_map/reduce_terms/pallas_call | solution.py:363
  155.2 1.2 maximum_bitcast_fusion
  156.4 0.0 copy-start.9
  156.4 0.9 fusion.87
  157.3 2.6 %multiply_reduce_fusion = (f32[384]{0:T(512)S(1)}, f32[384,1280]{1,0:T(8,128)S(1)}) fusion(f32[384,1280]{1,0:T(8,128)S(1)} %copy-done.4, f32[384]{0:T(512)S(1)} %broadcast_multiply_fusion.2, f32[384,1280]{1,0:T(8,128)S(1)} %get-tuple-element.44, f32[1280]{0:T(1024)S(1)} %copy-done.11, f32[384]{0:T(512)S(1)} %fusion.74, ...), kind=kOutput, calls=%fused_computation.11 | convolution fusion | flops 638484096 | bytes 8037888 | tf_op jit(solution)/shard_map/dot_general | solution.py:41
  160.0 0.0 slice-start
  160.0 0.0 copy-start.10
  160.0 2.7 %fusion.83 = (f32[384]{0:T(512)S(1)}, f32[384,1280]{1,0:T(8,128)}) fusion(f32[384]{0:T(512)S(1)} %multiply_multiply_fusion.18, f32[384,1280]{1,0:T(8,128)S(1)} %get-tuple-element.67, f32[384,1280]{1,0:T(8,128)S(1)} %get-tuple-element.44, f32[1280]{0:T(1024)S(1)} %copy-done.11, f32[384]{0:T(512)S(1)} %fusion.74, f32[384,1280]{1,0:T(8,128)S(1)} %copy-done.4, ...), kind=kLoop, calls=%fused_computation.173 | loop fusion | flops 10813056 | bytes 7875584 | tf_op jit(solution)/shard_map/transpose(jvp())/reduce_sum | solution.py:19
  162.7 1.8 %copy.35 = f32[160,160]{1,0:T(8,128)} copy(f32[160,160]{0,1:T(8,128)} %get-tuple-element.46) | data formatting | bytes 204800
  164.5 0.9 copy.34
  165.4 0.8 copy.36
  166.2 2.8 %add_convert_fusion = bf16[384,1280]{1,0:T(8,128)(2,1)} fusion(f32[384,1280]{1,0:T(8,128)} %get-tuple-element.38, bf16[384,1280]{1,0:T(8,128)(2,1)S(1)} %copy-done.7, f32[384]{0:T(512)S(1)} %negate_multiply_fusion.3), kind=kLoop, calls=%fused_computation.10 | loop fusion | flops 1966080 | bytes 3933696 | tf_op jit(solution)/shard_map/convert_element_type | solution.py:100
  (37 shorter events, 0.2 us)
Async XLA Ops:
  0.6 64.3 %copy-start = (bf16[1280,640]{1,0:T(8,128)(2,1)S(1)}, bf16[1280,640]{1,0:T(8,128)(2,1)}, u32[]{:S(2)}) copy-start(bf16[1280,640]{1,0:T(8,128)(2,1)} %param.23) | copy-start | bytes 4915204
  8.5 49.2 %all-to-all-start = ((bf16[8,88,1280]{2,1,0:T(8,128)(2,1)}), bf16[8,88,1280]{2,1,0:T(8,128)(2,1)S(1)}, u32[]{:S(2)}, u32[]{:S(2)}) async-start(bf16[8,88,1280]{2,1,0:T(8,128)(2,1)} %select_convert_fusion), calls=%async_computation | async-start | bytes 3604480 | tf_op jit(solution)/shard_map/all_to_all | solution.py:311
  59.3 5.6 %copy-start.3 = (f32[384,1280]{1,0:T(8,128)}, f32[384,1280]{1,0:T(8,128)S(1)}, u32[]{:S(2)}) copy-start(f32[384,1280]{1,0:T(8,128)S(1)} %get-tuple-element.57) | copy-start | bytes 5898244
  59.3 0.7 copy-start.11
  65.0 1.1 copy-start.8
  65.0 1.3 copy-start.13
  66.3 2.9 %copy-start.5 = (bf16[640,5,640]{2,0,1:T(8,128)(2,1)S(1)}, bf16[640,5,640]{2,0,1:T(8,128)(2,1)}, u32[]{:S(2)}) copy-start(bf16[640,5,640]{2,0,1:T(8,128)(2,1)} %param.25) | copy-start | bytes 12288004
  69.0 1.5 copy-start.1
  71.8 1.1 copy-start.12
  72.6 3.7 %copy-start.6 = (bf16[384,1280]{1,0:T(8,128)(2,1)S(1)}, bf16[384,1280]{1,0:T(8,128)(2,1)}, u32[]{:S(2)}) copy-start(bf16[384,1280]{1,0:T(8,128)(2,1)} %upstream.1) | copy-start | bytes 2949124
  72.6 3.7 %copy-start.14 = (bf16[1280,640]{1,0:T(8,128)(2,1)S(1)}, bf16[1280,640]{1,0:T(8,128)(2,1)}, u32[]{:S(2)}) copy-start(bf16[1280,640]{1,0:T(8,128)(2,1)} %param.27) | copy-start | bytes 4915204
  78.8 4.6 %copy-start.2 = (bf16[384,640]{1,0:T(8,128)(2,1)}, bf16[384,640]{1,0:T(8,128)(2,1)S(1)}, u32[]{:S(2)}) copy-start(bf16[384,640]{1,0:T(8,128)(2,1)S(1)} %add_convert_fusion.2.conv_cot) | copy-start | bytes 1474564
  155.2 2.1 %copy-start.4 = (f32[384,1280]{1,0:T(8,128)S(1)}, f32[384,1280]{1,0:T(8,128)}, u32[]{:S(2)}) copy-start(f32[384,1280]{1,0:T(8,128)} %copy-done.3) | copy-start | bytes 5898244
  156.4 3.5 %copy-start.9 = (f32[768,160]{0,1:T(8,128)}, f32[768,160]{0,1:T(8,128)S(1)}, u32[]{:S(2)}) copy-start(f32[768,160]{0,1:T(8,128)S(1)} %maximum_bitcast_fusion) | copy-start | bytes 1474564
  160.0 4.5 %slice-start = ((f32[768,160]{0,1:T(8,128)}), f32[400,160]{0,1:T(8,128)S(1)}, s32[]{:S(2)}) async-start(f32[768,160]{0,1:T(8,128)} %copy-done.9), calls=%async_computation.1 | async-start | bytes 655360 | tf_op jit(solution)/shard_map/slice | solution.py:378
  160.0 5.4 %copy-start.10 = (f32[160,160]{0,1:T(8,128)S(1)}, f32[160,160]{0,1:T(8,128)}, u32[]{:S(2)}) copy-start(f32[160,160]{0,1:T(8,128)} %get-tuple-element.45) | copy-start | bytes 307204
  162.7 3.5 %copy-start.7 = (bf16[384,1280]{1,0:T(8,128)(2,1)S(1)}, bf16[384,1280]{1,0:T(8,128)(2,1)}, u32[]{:S(2)}) copy-start(bf16[384,1280]{1,0:T(8,128)(2,1)} %upstream.1) | copy-start | bytes 2949124

commit v2 on v1

v2 whole, which is shorter than its diff:
```python
import jax
import jax.numpy as jnp
from jax import lax
from jax.experimental import pallas as pl
from jax.experimental.pallas import tpu as pltpu
import functools
from jax.sharding import PartitionSpec as P

KERNEL_TAPS = 5
DILATION_STEP = 16
LMAX = 80


EPS = 1e-05


def normalized_activation(values, gain_vec):
    row_mean = jnp.mean(values, axis=-1, keepdims=True)
    centred = values - row_mean
    row_var = jnp.mean(centred * centred, axis=-1, keepdims=True)
    return jax.nn.gelu(centred * lax.rsqrt(row_var + EPS) * gain_vec, approximate=False)


def raw_shift(values, offset):
    if offset > 0:
        filler = jnp.zeros((offset, values.shape[1]), values.dtype)
        return jnp.concatenate([values[offset:], filler], axis=0)
    if offset < 0:
        filler = jnp.zeros((-offset, values.shape[1]), values.dtype)
        return jnp.concatenate([filler, values[:offset]], axis=0)
    return values


def contract_rows(left, right):
    return lax.dot_general(
        left, right, (((0,), (0,)), ((), ())), preferred_element_type=jnp.float32
    )


def contract_cols(left, right):
    return lax.dot_general(
        left, right, (((1,), (1,)), ((), ())), preferred_element_type=jnp.float32
    )


def layer_grads(
    owner_input,
    upstream,
    owner_position,
    owner_length,
    gain_in,
    weight_in,
    gain_mid,
    weight_conv,
    gain_out,
    weight_out,
):
    widened_input = owner_input.astype(jnp.float32)
    first_f32 = normalized_activation(widened_input, gain_in)
    first_act = first_f32.astype(jnp.bfloat16)
    hidden = jnp.dot(first_act, weight_in, preferred_element_type=jnp.float32)
    mid_f32, pull_mid = jax.vjp(lambda value: normalized_activation(value, gain_mid), hidden)
    mid_act = mid_f32.astype(jnp.bfloat16)
    tap_offsets = [
        (kernel_tap_index - KERNEL_TAPS // 2) * DILATION_STEP
        for kernel_tap_index in range(KERNEL_TAPS)
    ]
    tap_valid = [
        (owner_position + offset >= 0) & (owner_position + offset < owner_length)
        for offset in tap_offsets
    ]
    tap_list = [
        jnp.where(
            tap_valid[kernel_tap_index][:, None],
            raw_shift(mid_act, tap_offsets[kernel_tap_index]),
            jnp.zeros_like(mid_act),
        )
        for kernel_tap_index in range(KERNEL_TAPS)
    ]
    conv = jnp.dot(tap_list[0], weight_conv[:, 0, :], preferred_element_type=jnp.float32)
    for kernel_tap_index in range(1, KERNEL_TAPS):
        conv = conv + jnp.dot(
            tap_list[kernel_tap_index],
            weight_conv[:, kernel_tap_index, :],
            preferred_element_type=jnp.float32,
        )
    out_f32, pull_out = jax.vjp(lambda value: normalized_activation(value, gain_out), conv)
    out_act = out_f32.astype(jnp.bfloat16)
    out_cot = jnp.dot(upstream, weight_out, preferred_element_type=jnp.float32)
    conv_cot = pull_out(out_cot)[0].astype(jnp.bfloat16)
    mid_cot = jnp.zeros(mid_act.shape, jnp.float32)
    for kernel_tap_index in range(KERNEL_TAPS):
        back_term = contract_cols(conv_cot, weight_conv[:, kernel_tap_index, :])
        back_term = jnp.where(
            tap_valid[kernel_tap_index][:, None], back_term, jnp.zeros_like(back_term)
        )
        mid_cot = mid_cot + raw_shift(back_term, -tap_offsets[kernel_tap_index])
    hidden_cot = pull_mid(mid_cot)[0].astype(jnp.bfloat16)
    return (first_act, mid_act, out_act, conv_cot, hidden_cot)


MESH = pl.DeviceIdType.MESH


def bit_orders(owners, groups):
    dp_bits = [("dp", i) for i in range(owners.bit_length() - 1)]
    sh_bits = [("shard", i) for i in range(groups.bit_length() - 1)]
    first, others = sh_bits[:1], sh_bits[1:]
    return (
        first + others + dp_bits,
        first + dp_bits[:1] + others + dp_bits[1:],
        first + dp_bits[1:] + others + dp_bits[:1],
    )


def chunk_rows(rows):
    unit = rows // 5
    return (2 * unit, 2 * unit, unit)


def round_up(value, multiple):
    return -(-value // multiple) * multiple


def placed(values, offset):
    low = offset // 128 * 128
    high = round_up(offset + values.shape[1], 128)
    parts = []
    if offset > low:
        parts.append(jnp.zeros((values.shape[0], offset - low), values.dtype))
    parts.append(values)
    if high > offset + values.shape[1]:
        parts.append(jnp.zeros((values.shape[0], high - offset - values.shape[1]), values.dtype))
    return low, (jnp.concatenate(parts, axis=1) if len(parts) > 1 else values)


FILL = 64.0
INV_SQRT2 = 0.7071067811865476
INV_SQRT_2PI = 0.3989422804014327
VMEM_LIMIT = 60 * 1024 * 1024


def flipped(index, mask):
    other, bit = index, 0
    while (mask >> bit) > 0:
        if (mask >> bit) & 1:
            other = other + (1 - 2 * lax.rem(index // (1 << bit), 2)) * (1 << bit)
        bit += 1
    return other


def dispatch_kernel(
    owners,
    destination,
    position,
    order,
    timestep,
    token,
    embedded,
    bucket,
    bucket_pos,
    bucket_len,
    sent,
    got,
    send_sem,
    recv_sem,
):
    me, group = lax.axis_index("dp"), lax.axis_index("shard")
    barrier = pltpu.get_barrier_semaphore()
    for j in range(1, owners):
        pl.semaphore_signal(
            barrier, inc=1, device_id=(flipped(me, j), group), device_id_type=MESH
        )
    slot = jnp.where(destination[...] < owners, destination[...] * LMAX + position[...], -1)
    hidden_slot = (order[...] < timestep[...]).astype(jnp.float32)

    def block_for(owner):
        rows = lax.broadcasted_iota(jnp.int32, (LMAX, slot.shape[1]), 0) + owner * LMAX
        pick = (rows == slot).astype(jnp.float32)
        live = jnp.sum(pick, axis=1, keepdims=True)
        masked = jnp.sum(pick * hidden_slot, axis=1, keepdims=True)
        block = jnp.dot(
            pick.astype(jnp.bfloat16), embedded[...], preferred_element_type=jnp.float32
        )
        block = jnp.where(masked > 0.5, token[...].astype(jnp.float32), block)
        return jnp.where(live > 0.5, block, FILL).astype(jnp.bfloat16)

    copies = []
    for j in range(owners - 1, 0, -1):
        other = flipped(me, j)
        sent[j] = block_for(other)
        if j == owners - 1:
            pl.semaphore_wait(barrier, owners - 1)
        copy = pltpu.make_async_remote_copy(
            src_ref=sent.at[j],
            dst_ref=got.at[me],
            send_sem=send_sem.at[j],
            recv_sem=recv_sem.at[j],
            device_id=(other, group),
            device_id_type=MESH,
        )
        copy.start()
        copies.append(copy)
    got[me] = block_for(me)
    for copy in copies:
        copy.wait_recv()
    lanes = lax.broadcasted_iota(jnp.int32, (1, owners * LMAX), 1)
    place_of = jnp.full((1, owners * LMAX), -1, jnp.int32)
    pos_of = jnp.zeros((1, owners * LMAX), jnp.float32)
    len_of = jnp.zeros((1, owners * LMAX), jnp.float32)
    start = jnp.zeros((1, 1), jnp.int32)
    for source in range(owners):
        marks = got[source, :, 0:128].astype(jnp.float32)[:, 0:1]
        count = jnp.sum((marks < FILL / 2).astype(jnp.float32), axis=0, keepdims=True)
        whole = count.astype(jnp.int32)
        inside = lanes - source * LMAX
        used = (inside >= 0) & (inside < whole)
        place_of = jnp.where(used, start + inside, place_of)
        pos_of = jnp.where(used, inside.astype(jnp.float32), pos_of)
        len_of = jnp.where(used, count, len_of)
        start = start + whole
    own = bucket.shape[0]
    take = (
        lax.broadcasted_iota(jnp.int32, (own, owners * LMAX), 0) == place_of
    ).astype(jnp.float32)
    bucket_pos[...] = jnp.sum(take * pos_of, axis=1, keepdims=True).astype(jnp.int32)
    bucket_len[...] = jnp.sum(take * len_of, axis=1, keepdims=True).astype(jnp.int32)
    bucket[...] = jnp.dot(
        take.astype(jnp.bfloat16),
        got[...].reshape(owners * LMAX, bucket.shape[1]),
        preferred_element_type=jnp.float32,
    ).astype(jnp.bfloat16)
    for copy in copies:
        copy.wait_send()


def gradient_kernel(
    owners,
    groups,
    position,
    length,
    mid,
    conv_cot,
    first,
    hidden_cot,
    upstream,
    out_act,
    weight_in,
    owner_input,
    gain_in,
    grad_input,
    grad_in,
    grad_conv,
    grad_out,
    *scratch,
):
    chunks = 3
    terms, got, sums = scratch[:chunks], scratch[chunks : 2 * chunks], scratch[2 * chunks : 9]
    lefts, rights, input_cot, send_sem, recv_sem = (
        scratch[9:12],
        scratch[12:15],
        scratch[15],
        scratch[16],
        scratch[17],
    )
    orders = bit_orders(owners, groups)
    steps = len(orders[0])
    total = 1 << steps
    me = {"dp": lax.axis_index("dp"), "shard": lax.axis_index("shard")}

    def bit_of(axis, bit):
        return lax.rem(me[axis] // (1 << bit), 2)

    def partner(axis, bit):
        other = me[axis] + (1 - 2 * bit_of(axis, bit)) * (1 << bit)
        return (other, me["shard"]) if axis == "dp" else (me["dp"], other)

    barrier = pltpu.get_barrier_semaphore()
    for axis, bit in orders[0]:
        pl.semaphore_signal(barrier, inc=1, device_id=partner(axis, bit), device_id_type=MESH)

    narrow, wide = mid.shape[1] // owners, first.shape[1] // owners
    rows = conv_cot.shape[1] // groups
    width = terms[0].shape[2]
    offsets = (0, KERNEL_TAPS * narrow, KERNEL_TAPS * narrow + wide)
    taps = []
    for k in range(KERNEL_TAPS):
        offset = (k - KERNEL_TAPS // 2) * DILATION_STEP
        moved = position[...] + offset
        valid = (moved >= 0) & (moved < length[...])
        shifted = raw_shift(mid[...], offset).astype(jnp.float32)
        taps.append(jnp.where(valid, shifted, 0.0))
    for right, values in zip(rights, (conv_cot, hidden_cot, out_act)):
        right[...] = values[...].T
    for owner in range(owners):
        here = slice(owner * narrow, (owner + 1) * narrow)
        there = slice(owner * wide, (owner + 1) * wide)
        parts = (
            jnp.concatenate([t[:, here] for t in taps], axis=1),
            first[:, there].astype(jnp.float32),
            upstream[:, there].astype(jnp.float32),
        )
        for left, values, offset in zip(lefts, parts, offsets):
            left[owner] = placed(values, offset)[1].astype(jnp.bfloat16)

    def half_terms(low_bit):
        starts = [(2 * i + low_bit) * rows for i in range(groups // 2)]

        def body(owner, carry):
            tiles = [None] * (width // 128)
            for left, right, offset in zip(lefts, rights, offsets):
                low = offset // 128
                picked = [right[pl.ds(pl.multiple_of(s, 16), rows), :] for s in starts]
                picked = picked[0] if len(picked) == 1 else jnp.concatenate(picked, axis=0)
                term = jnp.dot(picked, left[owner], preferred_element_type=jnp.float32)
                for j in range(left.shape[2] // 128):
                    piece = term[:, j * 128 : (j + 1) * 128]
                    held = tiles[low + j]
                    tiles[low + j] = piece if held is None else held + piece
            for j, tile in enumerate(tiles):
                tile = tile.astype(jnp.bfloat16)
                for i in range(groups // 2):
                    at = i * rows
                    for order, out in zip(orders, terms):
                        index = low_bit
                        for axis, bit in order[1:]:
                            if axis == "dp":
                                index = index * 2 + lax.rem(owner // (1 << bit), 2)
                            else:
                                index = index * 2 + (((2 * i) >> bit) & 1)
                        count = out.shape[1]
                        out[index, :, j * 128 : (j + 1) * 128] = tile[at : at + count]
                        at += count
            return carry

        lax.fori_loop(0, owners, body, 0)

    base, at = [], 0
    for t in range(steps):
        base.append(at)
        at += total >> (t + 1)

    def copy_of(c, t):
        half = total >> (t + 1)
        away = 1 - bit_of(*orders[c][t])
        source = terms[c] if t == 0 else sums[c]
        start = away * half if t == 0 else base[t - 1] + away * half
        return pltpu.make_async_remote_copy(
            src_ref=source.at[pl.ds(start, half)],
            dst_ref=got[c].at[pl.ds(base[t], half)],
            send_sem=send_sem.at[c, t],
            recv_sem=recv_sem.at[c, t],
            device_id=partner(*orders[c][t]),
            device_id_type=MESH,
        )

    def summed(c, t, at):
        half = total >> (t + 1)
        kept = bit_of(*orders[c][t]) * half
        source = terms[c] if t == 0 else sums[c]
        offset = kept if t == 0 else base[t - 1] + kept
        return source[offset + at].astype(jnp.float32) + got[c][base[t] + at].astype(jnp.float32)

    def add(c, t, first_block, count):
        def body(i, carry):
            at = first_block + i
            sums[c][base[t] + at] = summed(c, t, at).astype(jnp.bfloat16)
            return carry

        lax.fori_loop(0, count, body, 0)

    def input_gradient():
        input_cot[...] = contract_cols(hidden_cot[...], weight_in[...])
        step_rows = 16

        def body(i, carry):
            at = pl.ds(pl.multiple_of(i * step_rows, step_rows), step_rows)
            value = owner_input[at, :].astype(jnp.float32)
            centred = value - jnp.mean(value, axis=-1, keepdims=True)
            scale = lax.rsqrt(jnp.mean(centred * centred, axis=-1, keepdims=True) + EPS)
            normal = centred * scale
            gain = gain_in[...]
            scaled = normal * gain
            slope = 0.5 * (1.0 + lax.erf(scaled * INV_SQRT2)) + scaled * (
                INV_SQRT_2PI * jnp.exp(-0.5 * scaled * scaled)
            )
            cot = input_cot[at, :] * slope * gain
            grad = scale * (
                cot
                - jnp.mean(cot, axis=-1, keepdims=True)
                - normal * jnp.mean(cot * normal, axis=-1, keepdims=True)
            )
            grad_input[at, :] = (upstream[at, :].astype(jnp.float32) + grad).astype(
                jnp.bfloat16
            )
            return carry

        lax.fori_loop(0, owner_input.shape[0] // step_rows, body, 0)

    mine = bit_of(*orders[0][0])
    half_terms(1 - mine)
    pl.semaphore_wait(barrier, steps)
    copies = [[copy_of(c, t) for t in range(steps)] for c in range(chunks)]
    for c in range(chunks):
        copies[c][0].start()
    half_terms(mine)
    for t in range(steps - 1):
        half = total >> (t + 2)
        for c in range(chunks):
            copies[c][t].wait_recv()
            nxt = bit_of(*orders[c][t + 1])
            add(c, t, (1 - nxt) * half, half)
            copies[c][t + 1].start()
            add(c, t, nxt * half, half)
        if t == 0:
            input_gradient()
    finished = []
    for c in range(chunks):
        copies[c][steps - 1].wait_recv()
        finished.append(summed(c, steps - 1, 0))
    result = jnp.concatenate(finished, axis=0).T
    for k in range(KERNEL_TAPS):
        grad_conv[:, k, :] = result[k * narrow : (k + 1) * narrow]
    grad_in[...] = result[offsets[1] : offsets[1] + wide]
    grad_out[...] = result[offsets[2] : offsets[2] + wide]
    for c in range(chunks):
        for t in range(steps):
            copies[c][t].wait_send()


def local(
    embedded,
    mask_token_embedding,
    destination,
    position,
    length,
    unmask_order,
    timestep,
    upstream,
    gain_in,
    weight_in,
    gain_mid,
    weight_conv,
    gain_out,
    weight_out,
):
    channels = embedded.shape[1]
    owners, groups = lax.axis_size("dp"), lax.axis_size("shard")
    own_rows = upstream.shape[0]
    inner = weight_in.shape[1]
    vmem = pl.BlockSpec(memory_space=pltpu.VMEM)
    bucket, bucket_pos, bucket_len = pl.pallas_call(
        functools.partial(dispatch_kernel, owners),
        out_shape=[
            jax.ShapeDtypeStruct((own_rows, channels), jnp.bfloat16),
            jax.ShapeDtypeStruct((own_rows, 1), jnp.int32),
            jax.ShapeDtypeStruct((own_rows, 1), jnp.int32),
        ],
        in_specs=[vmem] * 6,
        out_specs=[vmem] * 3,
        scratch_shapes=[
            pltpu.VMEM((owners, LMAX, channels), jnp.bfloat16),
            pltpu.VMEM((owners, LMAX, channels), jnp.bfloat16),
            pltpu.SemaphoreType.DMA((owners,)),
            pltpu.SemaphoreType.DMA((owners,)),
        ],
        compiler_params=pltpu.CompilerParams(
            collective_id=1, has_side_effects=True, vmem_limit_bytes=VMEM_LIMIT
        ),
        name="dispatch",
    )(
        destination[None, :],
        position[None, :],
        unmask_order[None, :],
        timestep[None, :],
        mask_token_embedding[None, :],
        embedded,
    )
    first_act, mid_act, out_act, conv_cot, hidden_cot = layer_grads(
        bucket,
        upstream,
        bucket_pos[:, 0],
        bucket_len[:, 0],
        gain_in,
        weight_in,
        gain_mid,
        weight_conv,
        gain_out,
        weight_out,
    )
    narrow, wide, rows = inner // owners, channels // owners, inner // groups
    offsets = (0, KERNEL_TAPS * narrow, KERNEL_TAPS * narrow + wide)
    sizes = (KERNEL_TAPS * narrow, wide, wide)
    spans = [round_up(o + n, 128) - o // 128 * 128 for o, n in zip(offsets, sizes)]
    width = round_up(offsets[2] + wide, 128)
    total = owners * groups
    steps = total.bit_length() - 1
    counts = chunk_rows(rows)
    outs = pl.pallas_call(
        functools.partial(gradient_kernel, owners, groups),
        out_shape=[
            jax.ShapeDtypeStruct((own_rows, channels), jnp.bfloat16),
            jax.ShapeDtypeStruct((wide, rows), jnp.float32),
            jax.ShapeDtypeStruct((narrow, KERNEL_TAPS, rows), jnp.float32),
            jax.ShapeDtypeStruct((wide, rows), jnp.float32),
        ],
        in_specs=[vmem] * 11,
        out_specs=[vmem] * 4,
        scratch_shapes=[pltpu.VMEM((total, n, width), jnp.bfloat16) for n in counts]
        + [pltpu.VMEM((total - 1, n, width), jnp.bfloat16) for n in counts]
        + [pltpu.VMEM((total - 1, n, width), jnp.bfloat16) for n in counts]
        + [pltpu.VMEM((owners, own_rows, n), jnp.bfloat16) for n in spans]
        + [pltpu.VMEM((inner, own_rows), jnp.bfloat16)] * 3
        + [pltpu.VMEM((own_rows, channels), jnp.float32)]
        + [pltpu.SemaphoreType.DMA((3, steps)), pltpu.SemaphoreType.DMA((3, steps))],
        compiler_params=pltpu.CompilerParams(
            collective_id=0, has_side_effects=True, vmem_limit_bytes=VMEM_LIMIT
        ),
        name="gradients",
    )(
        bucket_pos,
        bucket_len,
        mid_act,
        conv_cot,
        first_act,
        hidden_cot,
        upstream,
        out_act,
        weight_in,
        bucket,
        gain_in[None, :],
    )
    return tuple(outs)


def solution(mesh):
    return jax.shard_map(
        local,
        mesh=mesh,
        in_specs=(
            P(("dp", "shard"), None),
            P(),
            P(("dp", "shard")),
            P(("dp", "shard")),
            P(("dp", "shard")),
            P(("dp", "shard")),
            P(("dp", "shard")),
            P(("dp", "shard"), None),
            P(),
            P(),
            P(),
            P(),
            P(),
            P(),
        ),
        out_specs=(
            P(("dp", "shard"), None),
            P("dp", "shard"),
            P("dp", None, "shard"),
            P("dp", "shard"),
        ),
        check_vma=False,
    )
```

time: 171 us -> 147 us (0.86); the launches traced: 169 us -> 147 us
  waiting for transfers between devices: 41.9 us -> 0 us
  Pallas kernels: 67.2 us -> 108 us
  other arithmetic: 25.8 us -> 18.2 us
  matrix products: 19 us -> 11.4 us
  starting transfers between devices: 7.31 us -> 0 us
    all_to_all x1 -> x0, waiting for transfers between devices: 41.9 us -> none  [local(): got = lax.all_to_all(send, 'dp', split_axis=0, concat_axis=0, tiled=True)]
    pallas_call x2, Pallas kernels: 67.2 us -> 108 us  [the longest x1 60.3 us: local(): pl.pallas_call(functools.partial(gradient_kernel, owners, groups), out_sh...]
    all_to_all x1 -> x0, starting transfers between devices: 7.31 us -> none  [local(): got = lax.all_to_all(send, 'dp', split_axis=0, concat_axis=0, tiled=True)]
    dot_general x2 -> x0, matrix products: 5.07 us -> none  [the longest x1 3.99 us: local(): send = jnp.dot(pick, masked_input, preferred_element_type=jnp.float32)]
    convert_element_type x4 -> x0, other arithmetic: 4.46 us -> none  [the longest x1 2.78 us: layer_grads(): (upstream.astype(jnp.float32) + pull_in(input_cot)[0]).astype(jnp.bfloat16)]
    reduce_sum x3 -> x2, other arithmetic: 4.05 us -> 1.36 us  [normalized_activation(): centred = values - row_mean]
    dot_general x6 -> x5, matrix products: 8.25 us -> 5.64 us  [contract_cols(): lax.dot_general(left, right, (((1,), (1,)), ((), ())), preferred_element_...]
    pallas_call x0 -> x1, local copies, waits for them, and re-layouts: none -> 2.02 us  [local(): pl.pallas_call(functools.partial(gradient_kernel, owners, groups), out_sh...]
  transfers between devices with their start and end apart: 1 -> 0, of which waited for: 1 -> 0; matrix products, arithmetic and copies ran while one was open for 0% -> 0% of each run, Pallas kernels for 0% -> 0%
where the time goes in v2:
time: 147 us
  Pallas kernels  108 us (73%)
  other arithmetic  18.2 us (12%)
  matrix products  11.4 us (8%)
  local copies, waits for them, and re-layouts  7.94 us (5%)
    pallas_call x1, Pallas kernels, local(): pl.pallas_call(functools.partial(gradient_kernel, owners, groups), out_sh...  60.3 us
    pallas_call x1, Pallas kernels, local(): pl.pallas_call(functools.partial(dispatch_kernel, owners), out_shape=[jax...  48 us
    dot_general x5, matrix products, contract_cols(): lax.dot_general(left, right, (((1,), (1,)), ((), ())), preferred_element_...  5.64 us
    convert_element_type x1, other arithmetic, layer_grads(): first_act = first_f32.astype(jnp.bfloat16)  5.24 us
    unnamed x33, local copies, waits for them, and re-layouts  3.62 us
    convert_element_type x1, other arithmetic, layer_grads(): out_act = out_f32.astype(jnp.bfloat16)  3.36 us

profile of v2, /device:TPU:0, one launch (start us, length us, event | category | flops | bytes accessed | tf_op | source)
XLA Modules:
  0.0 146.7 jit_solution(11358491726921360367)
XLA Ops:
  0.6 0.0 copy-start
  0.6 1.4 broadcast_in_dim.109.token
  2.1 48.0 %dispatch.1 = (bf16[384,1280]{1,0:T(8,128)(2,1)}, s32[384,1]{1,0:T(8,128)}, s32[384,1]{1,0:T(8,128)}) custom-call(s32[1,960]{1,0:T(1,128)} %bitcast.46, s32[1,960]{1,0:T(1,128)} %bitcast.47, s32[1,960]{1,0:T(1,128)} %bitcast.48, s32[1,960]{1,0:T(1,128)} %bitcast.49, bf16[1,1280]{1,0:T(2,128)(2,1)} %broadcast_in_dim.109.token, bf16[960,1280]{1,0:T(8,128)(2,1)} %embedded.1), custom_call_target="tpu_custom_call" | custom-call | tf_op jit(solution)/shard_map/dispatch/pallas_call | solution.py:452
  50.0 0.0 copy-start.3
  50.0 0.0 copy-start.6
  50.0 1.6 %convert_reduce_fusion = f32[384]{0:T(512)S(1)} fusion(bf16[384,1280]{1,0:T(8,128)(2,1)} %get-tuple-element.9.owner_input), kind=kLoop, calls=%fused_computation.2 | loop fusion | flops 982656 | bytes 984576 | tf_op jit(solution)/shard_map/reduce_sum | solution.py:18
  51.6 1.6 %fusion.2 = f32[384]{0:T(512)S(1)} fusion(bf16[384,1280]{1,0:T(8,128)(2,1)} %get-tuple-element.9.owner_input, f32[384]{0:T(512)S(1)} %broadcast_multiply_fusion.2), kind=kLoop, calls=%fused_computation.5 | loop fusion | flops 1965696 | bytes 986112 | tf_op jit(solution)/shard_map/reduce_sum | solution.py:20
  53.2 0.0 copy-done.12
  53.2 0.0 copy-done.3
  53.2 5.2 %fusion.7.first = bf16[384,1280]{1,0:T(8,128)(2,1)S(1)} fusion(bf16[384,1280]{1,0:T(8,128)(2,1)S(1)} %copy-done.3, f32[1280]{0:T(1024)S(1)} %copy-done.12, f32[384]{0:T(512)S(1)} %add_rsqrt_fusion, f32[384]{0:T(512)S(1)} %broadcast_multiply_fusion.2), kind=kLoop, calls=%fused_computation.10 | loop fusion | flops 33914880 | bytes 1974272 | tf_op jit(solution)/shard_map/convert_element_type | solution.py:60
  58.5 0.0 copy-done.6
  58.5 0.0 copy-start.5
  58.5 0.0 copy-start.14
  58.5 1.0 fusion.91
  59.5 0.0 copy-done.5
  59.5 0.0 copy-start.8
  59.6 0.0 copy-start.9
  59.6 0.0 copy-start.4
  59.6 0.3 multiply_reduce_fusion.3
  59.8 0.0 copy-done.14
  59.9 2.7 %multiply_convert_fusion.1.mid = bf16[384,640]{1,0:T(8,128)(2,1)S(1)} fusion(f32[384,640]{1,0:T(8,128)S(1)} %get-tuple-element.34, f32[640]{0:T(1024)S(1)} %copy-done.14, f32[384]{0:T(512)S(1)} %fusion.79, f32[384]{0:T(512)S(1)} %broadcast_multiply_fusion.1), kind=kLoop, calls=%fused_computation.64 | loop fusion | flops 16711680 | bytes 1480192 | tf_op jit(solution)/shard_map/convert_element_type | solution.py:63
  62.5 0.0 copy-start.1
  62.6 0.1 fusion.89
  62.6 0.0 copy-done.8
  62.6 0.0 copy-done.9
  62.7 0.4 and_reduce_fusion
  63.0 0.0 copy-done.4
  63.0 0.7 fusion.48
  63.7 0.1 fusion.90
  63.8 0.7 convolution_add_fusion.3
  64.4 0.0 copy-done.1
  64.4 0.7 convolution_add_fusion.2
  65.1 0.6 convolution_add_fusion.1
  65.7 0.0 copy-start.13
  65.8 0.8 fusion.92
  66.5 0.3 multiply_reduce_fusion.2
  66.8 0.0 copy-done.13
  66.8 3.4 %multiply_convert_fusion = (bf16[384,640]{1,0:T(8,128)(2,1)}, f32[384,640]{1,0:T(8,128)S(1)}) fusion(f32[384,640]{1,0:T(8,128)S(1)} %get-tuple-element.36, f32[640]{0:T(1024)S(1)} %copy-done.13, f32[384]{0:T(512)S(1)} %fusion.80, f32[384]{0:T(512)S(1)} %broadcast_multiply_fusion), kind=kLoop, calls=%fused_computation.43 | loop fusion | flops 16711680 | bytes 2463232 | tf_op jit(solution)/shard_map/convert_element_type | solution.py:88
  70.2 0.0 copy-done
  70.2 0.0 copy-done.7
  70.2 1.4 multiply_reduce_fusion.1
  71.6 1.0 fusion.88
  72.5 0.1 add_convert_fusion.1.conv_cot
  72.7 0.0 copy-start.2
  72.7 0.6 fusion.38
  73.3 0.6 fusion.43
  73.9 0.1 slice.63
  74.0 0.2 slice_select_fusion
  74.2 0.6 fusion.35
  74.8 0.6 fusion.46
  75.4 0.1 slice.61
  75.5 0.2 slice_select_fusion.2
  75.7 0.0 copy-done.2
  75.7 3.2 %multiply_reduce_fusion = (f32[384]{0:T(512)S(1)}, f32[384,640]{1,0:T(8,128)S(1)}) fusion(f32[384,640]{1,0:T(8,128)S(1)} %get-tuple-element.34, f32[384]{0:T(512)S(1)} %broadcast_multiply_fusion.1, f32[352,640]{1,0:T(8,128)S(1)} %get-tuple-element.43, f32[368,640]{1,0:T(8,128)S(1)} %get-tuple-element.41, ...), kind=kOutput, calls=%fused_computation.45 | convolution fusion | flops 334724736 | bytes 6973440 | tf_op jit(solution)/shard_map/dot_general | solution.py:41
  78.9 0.4 fusion.87
  79.3 0.9 add_convert_fusion.hidden_cot
  80.3 0.6 broadcast_in_dim.124.gain_in
  80.9 60.3 %gradients.1 = (bf16[384,1280]{1,0:T(8,128)(2,1)}, f32[160,160]{1,0:T(8,128)}, f32[80,5,160]{2,1,0:T(8,128)}, f32[160,160]{1,0:T(8,128)}) custom-call(s32[384,1]{1,0:T(8,128)} %get-tuple-element.7.position, s32[384,1]{1,0:T(8,128)} %get-tuple-element.8.length, bf16[384,640]{1,0:T(8,128)(2,1)} %copy-done.1, bf16[384,640]{1,0:T(8,128)(2,1)} %copy-done.2, ...), custom_call_target="tpu_custom_call" | custom-call | tf_op jit(solution)/shard_map/gradients/pallas_call | solution.py:499
  141.1 0.0 copy-start.11
  141.1 0.0 copy-start.10
  141.2 2.0 %copy.18 = f32[80,5,160]{2,0,1:T(8,128)} copy(f32[80,5,160]{2,1,0:T(8,128)} %get-tuple-element.16) | data formatting | bytes 512000 | tf_op jit(solution)/shard_map/gradients/pallas_call | solution.py:499
  143.2 2.2 %copy.22 = bf16[384,1280]{1,0:T(8,128)(2,1)} copy(bf16[384,1280]{1,0:T(8,128)(2,1)} %get-tuple-element.49) | data formatting | bytes 1966080
  145.4 0.7 copy.23
  146.1 0.7 copy.24
  (14 shorter events, 0.1 us)
Async XLA Ops:
  0.6 69.6 %copy-start = (bf16[1280,640]{1,0:T(8,128)(2,1)S(1)}, bf16[1280,640]{1,0:T(8,128)(2,1)}, u32[]{:S(2)}) copy-start(bf16[1280,640]{1,0:T(8,128)(2,1)} %param.26) | copy-start | bytes 4915204
  2.1 51.2 %copy-start.12 = (f32[1280]{0:T(1024)S(1)}, f32[1280]{0:T(1024)}, u32[]{:S(2)}) copy-start(f32[1280]{0:T(1024)} %param.21) | copy-start | bytes 15364
  50.0 3.2 %copy-start.3 = (bf16[384,1280]{1,0:T(8,128)(2,1)S(1)}, bf16[384,1280]{1,0:T(8,128)(2,1)}, u32[]{:S(2)}) copy-start(bf16[384,1280]{1,0:T(8,128)(2,1)} %get-tuple-element.9.owner_input) | copy-start | bytes 2949124
  50.0 8.5 %copy-start.6 = (bf16[1280,640]{1,0:T(8,128)(2,1)S(1)}, bf16[1280,640]{1,0:T(8,128)(2,1)}, u32[]{:S(2)}) copy-start(bf16[1280,640]{1,0:T(8,128)(2,1)} %weight_in.1) | copy-start | bytes 4915204
  58.5 1.0 copy-start.5
  58.5 1.3 copy-start.14
  59.5 3.1 %copy-start.8 = (s32[384,1]{1,0:T(8,128)S(1)}, s32[384,1]{1,0:T(8,128)}, u32[]{:S(2)}) copy-start(s32[384,1]{1,0:T(8,128)} %get-tuple-element.7.position) | copy-start | bytes 4612
  59.6 3.1 %copy-start.9 = (s32[384,1]{1,0:T(8,128)S(1)}, s32[384,1]{1,0:T(8,128)}, u32[]{:S(2)}) copy-start(s32[384,1]{1,0:T(8,128)} %get-tuple-element.8.length) | copy-start | bytes 4612
  59.6 3.5 %copy-start.4 = (bf16[640,5,640]{2,0,1:T(8,128)(2,1)S(1)}, bf16[640,5,640]{2,0,1:T(8,128)(2,1)}, u32[]{:S(2)}) copy-start(bf16[640,5,640]{2,0,1:T(8,128)(2,1)} %param.24) | copy-start | bytes 12288004
  62.5 1.9 %copy-start.1 = (bf16[384,640]{1,0:T(8,128)(2,1)}, bf16[384,640]{1,0:T(8,128)(2,1)S(1)}, u32[]{:S(2)}) copy-start(bf16[384,640]{1,0:T(8,128)(2,1)S(1)} %multiply_convert_fusion.1.mid) | copy-start | bytes 1474564
  65.7 1.1 copy-start.13
  66.5 3.7 %copy-start.7 = (bf16[384,1280]{1,0:T(8,128)(2,1)S(1)}, bf16[384,1280]{1,0:T(8,128)(2,1)}, u32[]{:S(2)}) copy-start(bf16[384,1280]{1,0:T(8,128)(2,1)} %upstream.1) | copy-start | bytes 2949124
  72.7 3.0 %copy-start.2 = (bf16[384,640]{1,0:T(8,128)(2,1)}, bf16[384,640]{1,0:T(8,128)(2,1)S(1)}, u32[]{:S(2)}) copy-start(bf16[384,640]{1,0:T(8,128)(2,1)S(1)} %add_convert_fusion.1.conv_cot) | copy-start | bytes 1474564
  141.1 4.2 %copy-start.11 = (f32[160,160]{1,0:T(8,128)S(1)}, f32[160,160]{1,0:T(8,128)}, u32[]{:S(2)}) copy-start(f32[160,160]{1,0:T(8,128)} %get-tuple-element.50) | copy-start | bytes 307204
  141.1 4.9 %copy-start.10 = (f32[160,160]{1,0:T(8,128)S(1)}, f32[160,160]{1,0:T(8,128)}, u32[]{:S(2)}) copy-start(f32[160,160]{1,0:T(8,128)} %get-tuple-element.52) | copy-start | bytes 307204

commit v3 on v2

--- a/solution.py
+++ b/solution.py
@@ -44,23 +44,19 @@
 
 
 def layer_grads(
-    owner_input,
+    first_act,
+    mid_act,
     upstream,
     owner_position,
     owner_length,
-    gain_in,
     weight_in,
     gain_mid,
     weight_conv,
     gain_out,
     weight_out,
 ):
-    widened_input = owner_input.astype(jnp.float32)
-    first_f32 = normalized_activation(widened_input, gain_in)
-    first_act = first_f32.astype(jnp.bfloat16)
     hidden = jnp.dot(first_act, weight_in, preferred_element_type=jnp.float32)
-    mid_f32, pull_mid = jax.vjp(lambda value: normalized_activation(value, gain_mid), hidden)
-    mid_act = mid_f32.astype(jnp.bfloat16)
+    _, pull_mid = jax.vjp(lambda value: normalized_activation(value, gain_mid), hidden)
     tap_offsets = [
         (kernel_tap_index - KERNEL_TAPS // 2) * DILATION_STEP
         for kernel_tap_index in range(KERNEL_TAPS)
@@ -96,7 +92,7 @@
         )
         mid_cot = mid_cot + raw_shift(back_term, -tap_offsets[kernel_tap_index])
     hidden_cot = pull_mid(mid_cot)[0].astype(jnp.bfloat16)
-    return (first_act, mid_act, out_act, conv_cot, hidden_cot)
+    return (out_act, conv_cot, hidden_cot)
 
 
 MESH = pl.DeviceIdType.MESH
@@ -149,6 +145,13 @@
     return other
 
 
+def activated(value, gain):
+    centred = value - jnp.mean(value, axis=-1, keepdims=True)
+    scale = lax.rsqrt(jnp.mean(centred * centred, axis=-1, keepdims=True) + EPS)
+    scaled = centred * scale * gain
+    return 0.5 * scaled * (1.0 + lax.erf(scaled * INV_SQRT2))
+
+
 def dispatch_kernel(
     owners,
     destination,
@@ -157,11 +160,19 @@
     timestep,
     token,
     embedded,
+    gain_in,
+    weight_in,
+    gain_mid,
     bucket,
+    first,
+    mid,
     bucket_pos,
     bucket_len,
     sent,
     got,
+    got_first,
+    got_mid,
+    hidden,
     send_sem,
     recv_sem,
 ):
@@ -202,8 +213,33 @@
         copy.start()
         copies.append(copy)
     got[me] = block_for(me)
-    for copy in copies:
+
+    def forward(source):
+        step_rows = 16
+
+        def enter(i, carry):
+            at = pl.ds(pl.multiple_of(i * step_rows, step_rows), step_rows)
+            value = got[source, at, :].astype(jnp.float32)
+            got_first[source, at, :] = activated(value, gain_in[...]).astype(jnp.bfloat16)
+            return carry
+
+        def middle(i, carry):
+            at = pl.ds(pl.multiple_of(i * step_rows, step_rows), step_rows)
+            got_mid[source, at, :] = activated(hidden[at, :], gain_mid[...]).astype(
+                jnp.bfloat16
+            )
+            return carry
+
+        lax.fori_loop(0, LMAX // step_rows, enter, 0)
+        hidden[...] = jnp.dot(
+            got_first[source], weight_in[...], preferred_element_type=jnp.float32
+        )
+        lax.fori_loop(0, LMAX // step_rows, middle, 0)
+
+    forward(me)
+    for j, copy in zip(range(owners - 1, 0, -1), copies):
         copy.wait_recv()
+        forward(flipped(me, j))
     lanes = lax.broadcasted_iota(jnp.int32, (1, owners * LMAX), 1)
     place_of = jnp.full((1, owners * LMAX), -1, jnp.int32)
     pos_of = jnp.zeros((1, owners * LMAX), jnp.float32)
@@ -225,11 +261,13 @@
     ).astype(jnp.float32)
     bucket_pos[...] = jnp.sum(take * pos_of, axis=1, keepdims=True).astype(jnp.int32)
     bucket_len[...] = jnp.sum(take * len_of, axis=1, keepdims=True).astype(jnp.int32)
-    bucket[...] = jnp.dot(
-        take.astype(jnp.bfloat16),
-        got[...].reshape(owners * LMAX, bucket.shape[1]),
-        preferred_element_type=jnp.float32,
-    ).astype(jnp.bfloat16)
+    take = take.astype(jnp.bfloat16)
+    for result, blocks in ((bucket, got), (first, got_first), (mid, got_mid)):
+        result[...] = jnp.dot(
+            take,
+            blocks[...].reshape(owners * LMAX, result.shape[1]),
+            preferred_element_type=jnp.float32,
+        ).astype(jnp.bfloat16)
     for copy in copies:
         copy.wait_send()
 
@@ -420,7 +458,7 @@
         finished.append(summed(c, steps - 1, 0))
     result = jnp.concatenate(finished, axis=0).T
     for k in range(KERNEL_TAPS):
-        grad_conv[:, k, :] = result[k * narrow : (k + 1) * narrow]
+        grad_conv[k] = result[k * narrow : (k + 1) * narrow]
     grad_in[...] = result[offsets[1] : offsets[1] + wide]
     grad_out[...] = result[offsets[2] : offsets[2] + wide]
     for c in range(chunks):
@@ -449,18 +487,23 @@
     own_rows = upstream.shape[0]
     inner = weight_in.shape[1]
     vmem = pl.BlockSpec(memory_space=pltpu.VMEM)
-    bucket, bucket_pos, bucket_len = pl.pallas_call(
+    bucket, first_act, mid_act, bucket_pos, bucket_len = pl.pallas_call(
         functools.partial(dispatch_kernel, owners),
         out_shape=[
             jax.ShapeDtypeStruct((own_rows, channels), jnp.bfloat16),
+            jax.ShapeDtypeStruct((own_rows, channels), jnp.bfloat16),
+            jax.ShapeDtypeStruct((own_rows, inner), jnp.bfloat16),
             jax.ShapeDtypeStruct((own_rows, 1), jnp.int32),
             jax.ShapeDtypeStruct((own_rows, 1), jnp.int32),
         ],
-        in_specs=[vmem] * 6,
-        out_specs=[vmem] * 3,
+        in_specs=[vmem] * 9,
+        out_specs=[vmem] * 5,
         scratch_shapes=[
             pltpu.VMEM((owners, LMAX, channels), jnp.bfloat16),
             pltpu.VMEM((owners, LMAX, channels), jnp.bfloat16),
+            pltpu.VMEM((owners, LMAX, channels), jnp.bfloat16),
+            pltpu.VMEM((owners, LMAX, inner), jnp.bfloat16),
+            pltpu.VMEM((LMAX, inner), jnp.float32),
             pltpu.SemaphoreType.DMA((owners,)),
             pltpu.SemaphoreType.DMA((owners,)),
         ],
@@ -475,13 +518,16 @@
         timestep[None, :],
         mask_token_embedding[None, :],
         embedded,
-    )
-    first_act, mid_act, out_act, conv_cot, hidden_cot = layer_grads(
-        bucket,
+        gain_in[None, :],
+        weight_in,
+        gain_mid[None, :],
+    )
+    out_act, conv_cot, hidden_cot = layer_grads(
+        first_act,
+        mid_act,
         upstream,
         bucket_pos[:, 0],
         bucket_len[:, 0],
-        gain_in,
         weight_in,
         gain_mid,
         weight_conv,
@@ -501,7 +547,7 @@
         out_shape=[
             jax.ShapeDtypeStruct((own_rows, channels), jnp.bfloat16),
             jax.ShapeDtypeStruct((wide, rows), jnp.float32),
-            jax.ShapeDtypeStruct((narrow, KERNEL_TAPS, rows), jnp.float32),
+            jax.ShapeDtypeStruct((KERNEL_TAPS, narrow, rows), jnp.float32),
             jax.ShapeDtypeStruct((wide, rows), jnp.float32),
         ],
         in_specs=[vmem] * 11,
@@ -530,7 +576,7 @@
         bucket,
         gain_in[None, :],
     )
-    return tuple(outs)
+    return (outs[0], outs[1], outs[2].transpose(1, 0, 2), outs[3])
 
 
 def solution(mesh):

time: 147 us -> 155 us (1.054)
  Pallas kernels: 108 us -> 120 us
  other arithmetic: 18.2 us -> 8.27 us
  local copies, waits for them, and re-layouts: 7.94 us -> 12.8 us
    pallas_call x1, Pallas kernels: 48 us -> 59.7 us  [local(): pl.pallas_call(functools.partial(dispatch_kernel, owners), out_shape=[jax...]
    convert_element_type x2 -> x0, other arithmetic: 7.92 us -> none  [the longest x1 5.24 us: layer_grads(): first_act = first_f32.astype(jnp.bfloat16)]
    unnamed x33 -> x22, local copies, waits for them, and re-layouts: 3.62 us -> 7.38 us
    broadcast_in_dim x1 -> x2, local copies, waits for them, and re-layouts: 0.6 us -> 2.68 us  [the longest x1 1.42 us: local(): gain_in[None, :]]
    pallas_call x1 -> x0, local copies, waits for them, and re-layouts: 2.02 us -> none  [local(): pl.pallas_call(functools.partial(gradient_kernel, owners, groups), out_sh...]
    reduce_sum x3 -> x2, other arithmetic: 2.11 us -> 0.53 us  [normalized_activation(): row_var = jnp.mean(centred * centred, axis=-1, keepdims=True)]
    reduce_sum x1 -> x0, other arithmetic: 1.56 us -> none  [normalized_activation(): row_mean = jnp.mean(values, axis=-1, keepdims=True)]
where the time goes in v3:
time: 155 us
  Pallas kernels  120 us (77%)
  local copies, waits for them, and re-layouts  12.8 us (8%)
  matrix products  12.5 us (8%)
  other arithmetic  8.27 us (5%)
    pallas_call x1, Pallas kernels, local(): pl.pallas_call(functools.partial(gradient_kernel, owners, groups), out_sh...  60.4 us
    pallas_call x1, Pallas kernels, local(): pl.pallas_call(functools.partial(dispatch_kernel, owners), out_shape=[jax...  59.7 us
    unnamed x22, local copies, waits for them, and re-layouts  7.38 us
    dot_general x5, matrix products, contract_cols(): lax.dot_general(left, right, (((1,), (1,)), ((), ())), preferred_element_...  5.62 us
    convert_element_type x1, other arithmetic, layer_grads(): out_act = out_f32.astype(jnp.bfloat16)  3.35 us

profile of v3, /device:TPU:0, one launch (start us, length us, event | category | flops | bytes accessed | tf_op | source)
XLA Modules:
  0.0 154.6 jit_solution(9377895217880349068)
XLA Ops:
  0.6 0.0 copy-start
  0.6 1.4 broadcast_in_dim.111.gain_in
  2.1 1.3 broadcast_in_dim.110.token
  3.3 1.3 broadcast_in_dim.112.gain_mid
  4.6 59.7 %dispatch.1 = (bf16[384,1280]{1,0:T(8,128)(2,1)}, bf16[384,1280]{1,0:T(8,128)(2,1)}, bf16[384,640]{1,0:T(8,128)(2,1)}, s32[384,1]{1,0:T(8,128)}, s32[384,1]{1,0:T(8,128)}) custom-call(s32[1,960]{1,0:T(1,128)} %bitcast.48, s32[1,960]{1,0:T(1,128)} %bitcast.49, s32[1,960]{1,0:T(1,128)} %bitcast.50, s32[1,960]{1,0:T(1,128)} %bitcast.51, ...), custom_call_target="tpu_custom_call" | custom-call | tf_op jit(solution)/shard_map/dispatch/pallas_call | solution.py:490
  64.3 0.0 copy-start.2
  64.3 0.0 copy-start.3
  64.3 1.5 and_reduce_fusion
  65.9 1.2 fusion.75
  67.1 1.8 %fusion.34 = f32[384,640]{1,0:T(8,128)S(1)} fusion(bf16[640,5,640]{2,0,1:T(8,128)(2,1)} %param.24, bf16[352,640]{1,0:T(8,128)(2,1)S(1)} %get-tuple-element.34, pred[384]{0:T(512)(128)(4,1)S(1)} %get-tuple-element.26), kind=kOutput, calls=%fused_computation.73 | convolution fusion | flops 314818560 | bytes 2253184 | tf_op jit(solution)/shard_map/dot_general | solution.py:76
  68.9 0.0 copy-done.2
  68.9 0.1 fusion.76
  69.0 0.0 copy-done.3
  69.0 0.7 convolution_add_fusion.3
  69.7 0.7 convolution_add_fusion.2
  70.4 0.0 copy-start.7
  70.4 0.6 convolution_add_fusion.1
  71.0 0.0 copy-start.5
  71.0 0.8 fusion.77
  71.8 0.3 multiply_reduce_fusion.3
  72.1 0.0 copy-done.7
  72.1 3.3 %multiply_convert_fusion = (bf16[384,640]{1,0:T(8,128)(2,1)}, f32[384,640]{1,0:T(8,128)S(1)}) fusion(f32[384,640]{1,0:T(8,128)S(1)} %get-tuple-element.38, f32[640]{0:T(1024)S(1)} %copy-done.7, f32[384]{0:T(512)S(1)} %fusion.65, f32[384]{0:T(512)S(1)} %broadcast_multiply_fusion.1), kind=kLoop, calls=%fused_computation.18 | loop fusion | flops 16711680 | bytes 2463232 | tf_op jit(solution)/shard_map/convert_element_type | solution.py:84
  75.4 0.0 copy-done
  75.4 0.0 copy-done.5
  75.4 1.4 multiply_reduce_fusion.2
  76.8 1.0 fusion.74
  77.8 0.1 add_convert_fusion.1.conv_cot
  77.9 0.0 copy-start.1
  78.0 0.6 fusion.24
  78.6 0.6 fusion.29
  79.2 0.1 slice.59
  79.3 0.2 slice_select_fusion
  79.5 0.0 copy-start.4
  79.5 0.0 copy-start.6
  79.5 0.6 fusion.21
  80.1 0.6 fusion.32
  80.7 0.1 slice.57
  80.8 0.2 slice_select_fusion.2
  81.0 0.0 copy-start.8
  81.0 0.0 copy-done.4
  81.0 0.1 copy-done.6
  81.2 1.0 fusion.78
  82.2 0.3 multiply_reduce_fusion.1
  82.5 0.0 copy-done.1
  82.5 0.0 copy-done.8
  82.5 3.2 %multiply_reduce_fusion = (f32[384]{0:T(512)S(1)}, f32[384,640]{1,0:T(8,128)S(1)}) fusion(f32[384,640]{1,0:T(8,128)S(1)} %get-tuple-element.42, f32[384]{0:T(512)S(1)} %broadcast_multiply_fusion, f32[352,640]{1,0:T(8,128)S(1)} %get-tuple-element.47, f32[368,640]{1,0:T(8,128)S(1)} %get-tuple-element.45, bf16[384,640]{1,0:T(8,128)(2,1)S(1)} %add_convert_fusion.1.conv_cot, ...), kind=kOutput, calls=%fused_computation.20 | convolution fusion | flops 334724736 | bytes 6973440 | tf_op jit(solution)/shard_map/dot_general | solution.py:41
  85.7 0.4 fusion.73
  86.1 0.9 add_convert_fusion.hidden_cot
  87.0 60.4 %gradients.1 = (bf16[384,1280]{1,0:T(8,128)(2,1)}, f32[160,160]{1,0:T(8,128)}, f32[5,80,160]{2,1,0:T(8,128)}, f32[160,160]{1,0:T(8,128)}) custom-call(s32[384,1]{1,0:T(8,128)} %get-tuple-element.13.position, s32[384,1]{1,0:T(8,128)} %get-tuple-element.14.length, bf16[384,640]{1,0:T(8,128)(2,1)} %get-tuple-element.15.mid, bf16[384,640]{1,0:T(8,128)(2,1)} %copy-done.1, ...), custom_call_target="tpu_custom_call" | custom-call | tf_op jit(solution)/shard_map/gradients/pallas_call | solution.py:545
  147.4 2.2 %copy.21 = bf16[384,1280]{1,0:T(8,128)(2,1)} copy(bf16[384,1280]{1,0:T(8,128)(2,1)} %get-tuple-element.53) | data formatting | bytes 1966080
  149.7 1.6 %copy.22 = f32[160,160]{1,0:T(8,128)} copy(f32[160,160]{1,0:T(8,128)} %get-tuple-element.54) | data formatting | bytes 204800
  151.2 1.8 %copy.23 = f32[80,5,160]{2,0,1:T(8,128)} copy(f32[80,5,160]{2,0,1:T(8,128)} %bitcast.45) | data formatting | bytes 512000
  153.0 1.6 %copy.24 = f32[160,160]{1,0:T(8,128)} copy(f32[160,160]{1,0:T(8,128)} %get-tuple-element.56) | data formatting | bytes 204800
  (8 shorter events, 0.1 us)
Async XLA Ops:
  0.6 74.8 %copy-start = (bf16[1280,640]{1,0:T(8,128)(2,1)S(1)}, bf16[1280,640]{1,0:T(8,128)(2,1)}, u32[]{:S(2)}) copy-start(bf16[1280,640]{1,0:T(8,128)(2,1)} %param.26) | copy-start | bytes 4915204
  64.3 4.6 %copy-start.2 = (bf16[384,640]{1,0:T(8,128)(2,1)S(1)}, bf16[384,640]{1,0:T(8,128)(2,1)}, u32[]{:S(2)}) copy-start(bf16[384,640]{1,0:T(8,128)(2,1)} %get-tuple-element.15.mid) | copy-start | bytes 1474564
  64.3 4.7 %copy-start.3 = (bf16[640,5,640]{2,0,1:T(8,128)(2,1)S(1)}, bf16[640,5,640]{2,0,1:T(8,128)(2,1)}, u32[]{:S(2)}) copy-start(bf16[640,5,640]{2,0,1:T(8,128)(2,1)} %param.24) | copy-start | bytes 12288004
  70.4 1.7 %copy-start.7 = (f32[640]{0:T(1024)S(1)}, f32[640]{0:T(1024)}, u32[]{:S(2)}) copy-start(f32[640]{0:T(1024)} %param.25) | copy-start | bytes 7684
  71.0 4.4 %copy-start.5 = (bf16[384,1280]{1,0:T(8,128)(2,1)S(1)}, bf16[384,1280]{1,0:T(8,128)(2,1)}, u32[]{:S(2)}) copy-start(bf16[384,1280]{1,0:T(8,128)(2,1)} %upstream.1) | copy-start | bytes 2949124
  77.9 4.5 %copy-start.1 = (bf16[384,640]{1,0:T(8,128)(2,1)}, bf16[384,640]{1,0:T(8,128)(2,1)S(1)}, u32[]{:S(2)}) copy-start(bf16[384,640]{1,0:T(8,128)(2,1)S(1)} %add_convert_fusion.1.conv_cot) | copy-start | bytes 1474564
  79.5 1.5 copy-start.4
  79.5 1.7 %copy-start.6 = (bf16[384,1280]{1,0:T(8,128)(2,1)S(1)}, bf16[384,1280]{1,0:T(8,128)(2,1)}, u32[]{:S(2)}) copy-start(bf16[384,1280]{1,0:T(8,128)(2,1)} %get-tuple-element.16.first) | copy-start | bytes 2949124
  81.0 1.5 copy-start.8
